TPU v7x, 512 devices: a whole 4x8x8 slice. The times are simulated.
512 devices in a mesh: section: 8 (over x, core), seq: 64 (over z, y).
Axes of the slice: x: 4, y: 8, z: 8, core: 2. Of those that a mesh axis runs over, the one named last changes fastest.
Arguments:
- stream: bfloat16 [8, 8192, 4096], P('section', 'seq'), may hold values from -200 to 200
- cotangent: bfloat16 [8, 8192, 4096], P('section', 'seq'), may hold values from -24 to 24
- keys: bfloat16 [8, 8192, 512], P('section', 'seq'), may hold values from -30 to 30
- values: bfloat16 [8, 8192, 512], P('section', 'seq'), may hold values from -6 to 6
- gain: float32 [8, 4096], P('section'), may hold values from 0.5 to 2
- rand_blocks: int32 [64, 1], P('seq'), may hold values from 0 to 63, as said below
Outputs:
- stream_grads: bfloat16 [8, 8192, 4096], P('section', 'seq')
- key_grads: bfloat16 [8, 8192, 512], P('section', 'seq')
- value_grads: bfloat16 [8, 8192, 512], P('section', 'seq')
Inputs may be any that keep to these rules, and one draw needn't show every extreme that they name: `rand_blocks`: row d names one block, of the form d xor 2**b with b >= 1; every row d = 2**b with b >= 1 names block 0.
All inputs are finite; a program needn't handle non-finite values.
Results may differ from a plain program's by a relative error of at most 0.012.
The roundings to bfloat16 on the way count: a program that leaves them out, or rounds other values in their place, can miss the bound.
Values may be sent and summed in bfloat16 or wider, within the bound.
A program may use at most 128 MiB of HBM per device.

v0:
```python
import jax
import jax.numpy as jnp
from jax import lax
from jax.sharding import PartitionSpec as P

HD = 128
RAND = 1


def extended(array, sides, width):
    for axis, dim in sides:
        peers, length = (lax.axis_size(axis), array.shape[dim])
        up = [(i, (i + 1) % peers) for i in range(peers - 1)]
        down = [(j, i) for i, j in up]
        last = lax.slice_in_dim(array, length - width, length, axis=dim)
        leading = lax.slice_in_dim(array, 0, width, axis=dim)
        before = lax.ppermute(last, axis, up)
        after = lax.ppermute(leading, axis, down)
        array = jnp.concatenate([before, array, after], axis=dim)
    return array


def broadcast(value, axis, source):
    kept = jnp.where(lax.axis_index(axis) == source, value, 0).astype(value.dtype)
    return lax.psum(kept, axis)


def swapped(value, axis, apart):
    mask = 2**apart
    pairs = [(source, source ^ mask) for source in range(lax.axis_size(axis))]
    return lax.ppermute(value, axis, pairs)


def from_behind(block, axis, distance):
    devices = range(lax.axis_size(axis))
    route = [((i - distance) % len(devices), i) for i in devices]
    return lax.ppermute(block, axis, route)


def from_behind_2(block, axis, distance):
    devices = range(lax.axis_size(axis))
    route = [(i - distance, i) for i in devices if i - distance in devices]
    return lax.ppermute(block, axis, route)


def group_terms(queries, slot_keys, slot_values, slot_valid, upstream):
    row_count = queries.shape[0]
    head_dim = slot_keys.shape[1]
    head_count = queries.shape[1] // head_dim
    factor = head_dim ** (-0.5)
    query_heads = queries.reshape(row_count, head_count, head_dim)
    grad_heads = upstream.reshape(row_count, head_count, head_dim)
    scores = jnp.where(
        slot_valid[None, None, :],
        jnp.einsum("qhd,kd->hqk", query_heads, slot_keys, preferred_element_type=jnp.float32)
        * factor,
        -1e30,
    )
    row_peak = jnp.max(scores, axis=2, keepdims=True)
    raised = jnp.exp(scores - row_peak)
    weights = raised / jnp.sum(raised, axis=2, keepdims=True)
    weights_low = weights.astype(jnp.bfloat16)
    grad_weights = jnp.einsum(
        "qhd,kd->hqk", grad_heads, slot_values, preferred_element_type=jnp.float32
    )
    row_dot = jnp.sum(weights * grad_weights, axis=2, keepdims=True)
    grad_low = (weights * (grad_weights - row_dot) * factor).astype(jnp.bfloat16)
    grad_query = jnp.einsum("hqk,kd->qhd", grad_low, slot_keys, preferred_element_type=jnp.float32)
    grad_keys = jnp.einsum("hqk,qhd->kd", grad_low, query_heads, preferred_element_type=jnp.float32)
    grad_values = jnp.einsum(
        "hqk,qhd->kd", weights_low, grad_heads, preferred_element_type=jnp.float32
    )
    return (grad_query.reshape(row_count, head_count * head_dim), grad_keys, grad_values)


def on_device(stream, cotangent, keys, values, gain, rand_blocks):
    hidden = stream[0]
    upstream = cotangent[0]
    block_rows = hidden.shape[0]
    model_width = hidden.shape[1]
    kv_width = keys.shape[2]
    groups = kv_width // HD
    query_cols = model_width // groups
    seq_count = lax.axis_size("seq")
    bit_count = seq_count.bit_length() - 1
    device = lax.axis_index("seq")
    own_blocks = jnp.concatenate([keys[0], values[0]], axis=1)
    window = extended(own_blocks, (("seq", 0),), block_rows)
    global_block = broadcast(own_blocks, "seq", 0)
    partner_rows = []
    partner_ids = []
    for bit_index in range(1, bit_count):
        partner_rows.append(swapped(own_blocks, "seq", bit_index))
        partner_ids.append(jnp.bitwise_xor(device, 1 << bit_index))
    wanted = rand_blocks[0]
    slot_index = 0
    picked = jnp.zeros_like(own_blocks)
    for position in range(len(partner_rows)):
        picked = jnp.where(
            wanted[slot_index] == partner_ids[position], partner_rows[position], picked
        )
    chosen = [picked]
    slots = jnp.concatenate([window, global_block] + chosen, axis=0)
    flags = jnp.stack(
        [device > 0, device >= 0, device < seq_count - 1, device > 0] + [device >= 0] * RAND
    )
    slot_valid = jnp.repeat(flags, block_rows)
    hidden_wide = hidden.astype(jnp.float32)
    inverse = lax.rsqrt(jnp.mean(hidden_wide * hidden_wide, axis=1, keepdims=True) + 1e-05)
    normed = hidden_wide * inverse
    gain_row = gain[0]
    queries = (normed * gain_row).astype(jnp.bfloat16)
    query_parts = []
    key_parts = []
    value_parts = []
    for group in range(groups):
        grad_query, grad_keys, grad_values = group_terms(
            queries[:, group * query_cols : (group + 1) * query_cols],
            slots[:, group * HD : (group + 1) * HD],
            slots[:, kv_width + group * HD : kv_width + (group + 1) * HD],
            slot_valid,
            upstream[:, group * query_cols : (group + 1) * query_cols],
        )
        query_parts.append(grad_query)
        key_parts.append(grad_keys)
        value_parts.append(grad_values)
    grad_query = jnp.concatenate(query_parts, axis=1)
    grad_slots = jnp.concatenate(key_parts + value_parts, axis=1)
    grad_normed = grad_query * gain_row
    grad_hidden = inverse * (
        grad_normed - normed * jnp.mean(grad_normed * normed, axis=1, keepdims=True)
    )
    handed = (upstream.astype(jnp.float32) + grad_hidden).astype(jnp.bfloat16)
    previous = from_behind(handed, "section", -1)
    self_term = grad_slots[block_rows : 2 * block_rows]
    to_prev = grad_slots[0:block_rows].astype(jnp.bfloat16)
    to_next = grad_slots[2 * block_rows : 3 * block_rows].astype(jnp.bfloat16)
    global_term = grad_slots[3 * block_rows : 4 * block_rows]
    slot_index = 0
    random_terms = [
        grad_slots[(4 + slot_index) * block_rows : (5 + slot_index) * block_rows].astype(
            jnp.bfloat16
        )
    ]
    from_prev = from_behind_2(to_next, "seq", 1)
    from_next = from_behind_2(to_prev, "seq", -1)
    returned = jnp.zeros(self_term.shape, jnp.float32)
    for bit_index in range(1, bit_count):
        outgoing = jnp.zeros_like(to_prev)
        slot_index = 0
        outgoing = jnp.where(
            wanted[slot_index] == partner_ids[bit_index - 1], random_terms[slot_index], outgoing
        )
        returned = returned + swapped(outgoing, "seq", bit_index).astype(jnp.float32)
    local_total = (
        self_term + from_prev.astype(jnp.float32) + from_next.astype(jnp.float32) + returned
    )
    summed = lax.psum(global_term, "seq")
    total = (local_total + jnp.where(device == 0, summed, 0.0)).astype(jnp.bfloat16)
    return (previous[None], total[:, :kv_width][None], total[:, kv_width:][None])


def solution(mesh):
    return jax.shard_map(
        on_device,
        mesh=mesh,
        in_specs=(
            P("section", "seq", None),
            P("section", "seq", None),
            P("section", "seq", None),
            P("section", "seq", None),
            P("section", None),
            P("seq", None),
        ),
        out_specs=(P("section", "seq", None), P("section", "seq", None), P("section", "seq", None)),
        check_vma=False,
    )
```

profile of v0, /device:TPU:6, one launch (start us, length us, event | category | flops | bytes accessed | tf_op | source)
XLA Modules:
  0.0 463.9 jit_solution(14307888164185576298)
XLA Ops:
  7.2 1.8 pad_maximum_fusion
  9.0 4.3 collective-permute-start
  13.3 1.3 collective-permute-start.1
  14.6 14.6 %collective-permute-start.2 = (bf16[128,1024]{1,0:T(8,128)(2,1)}, bf16[128,1024]{1,0:T(8,128)(2,1)}, u32[]{:S(2)}, u32[]{:S(2)}) collective-permute-start(bf16[128,1024]{1,0:T(8,128)(2,1)} %pad_maximum_fusion), channel_id=1, source_target_pairs={{0,32},{1,33},{2,34},{3,35},{4,36},{5,37},{6,38},{7,39},{8,40},{9,... | collective-permute-start | bytes 786440 | tf_op jit(solution)/shard_map/ppermute | solution.py:31
  29.2 3.1 collective-permute-start.3
  32.3 3.4 collective-permute-start.4
  35.7 1.6 copy.45
  40.5 6.8 %collective-permute-start.5 = (bf16[128,1024]{1,0:T(8,128)(2,1)}, bf16[128,1024]{1,0:T(8,128)(2,1)}, u32[]{:S(2)}, u32[]{:S(2)}) collective-permute-start(bf16[128,1024]{1,0:T(8,128)(2,1)} %pad_maximum_fusion), channel_id=1, source_target_pairs={{0,4},{1,5},{2,6},{3,7},{4,0},{5,1},{6,2},{7,3},{8,12},{9,13},{10,... | collective-permute-start | bytes 786440 | tf_op jit(solution)/shard_map/ppermute | solution.py:31
  47.3 1.7 constant_dynamic-update-slice_fusion.3
  50.0 1.9 collective-permute-start.6
  52.6 1.7 constant_dynamic-update-slice_fusion.1
  54.3 142.1 %all-reduce.3.cloned.1.call-done = bf16[128,1024]{1,0:T(8,128)(2,1)} async-done(((bf16[128,1024]{1,0:T(8,128)(2,1)}), bf16[128,1024]{1,0:T(8,128)(2,1)}) %all-reduce.3.cloned.1.call-update) | async-done | bytes 262160 | tf_op jit(solution)/shard_map/psum | solution.py:25
  196.4 1.7 constant_dynamic-update-slice_fusion
  198.2 1.9 select_dynamic-update-slice_fusion
  200.1 3.0 fusion.125
  203.0 3.4 fusion.160
  206.4 5.8 %fusion.67 = f32[128,8,128]{2,0,1:T(8,128)} fusion(f32[640,128,8]{1,0,2:T(8,128)} %fusion.125, bf16[640,1024]{1,0:T(8,128)(2,1)} %select_dynamic-update-slice_fusion, f32[8,128,640]{1,2,0:T(8,128)} %get-tuple-element.32, f32[8,128]{1,0:T(8,128)S(1)} %get-tuple-element.31), kind=kOutput, calls=%fused_computation.86 | convolution fusion | flops 172361344 | bytes 11182080 | tf_op jit(solution)/shard_map/hqk,kd->qhd/dot_general | solution.py:68
  212.2 5.7 %fusion.109 = f32[640,1024]{1,0:T(8,128)} fusion(bf16[128,8,128]{0,2,1:T(8,128)(2,1)S(1)} %bitcast.348, f32[640,128,8]{1,0,2:T(8,128)} %fusion.125, f32[8,128,640]{1,2,0:T(8,128)} %get-tuple-element.32, f32[8,128]{1,0:T(8,128)S(1)} %get-tuple-element.31), kind=kOutput, calls=%fused_computation.112 | convolution fusion | flops 172361344 | bytes 11083776 | tf_op jit(solution)/shard_map/hqk,qhd->kd/dot_general | solution.py:69
  217.9 3.0 fusion.122
  220.9 3.4 fusion.157
  224.3 2.9 fusion.123
  227.2 3.5 fusion.158
  230.7 2.9 fusion.124
  233.5 3.5 fusion.159
  237.0 5.8 %fusion.70 = f32[128,8,128]{2,0,1:T(8,128)} fusion(f32[640,128,8]{1,0,2:T(8,128)} %fusion.124, bf16[640,1024]{1,0:T(8,128)(2,1)} %select_dynamic-update-slice_fusion, f32[8,128,640]{1,2,0:T(8,128)} %get-tuple-element.30, f32[8,128]{1,0:T(8,128)S(1)} %get-tuple-element.29), kind=kOutput, calls=%fused_computation.89 | convolution fusion | flops 172361344 | bytes 11182080 | tf_op jit(solution)/shard_map/hqk,kd->qhd/dot_general | solution.py:68
  242.8 5.7 %fusion.107 = f32[640,1024]{1,0:T(8,128)} fusion(f32[640,1024]{1,0:T(8,128)} %fusion.109, bf16[128,8,128]{0,2,1:T(8,128)(2,1)} %bitcast.346, f32[640,128,8]{1,0,2:T(8,128)} %fusion.124, f32[8,128,640]{1,2,0:T(8,128)} %get-tuple-element.30, f32[8,128]{1,0:T(8,128)S(1)} %get-tuple-element.29), kind=kOutput, calls=%fused_computation.110 | convolution fusion | flops 172361344 | bytes 11083776 | tf_op jit(solution)/shard_map/hqk,qhd->kd/dot_general | solution.py:69
  248.5 5.8 %fusion.73 = f32[128,8,128]{2,0,1:T(8,128)} fusion(f32[640,128,8]{1,0,2:T(8,128)} %fusion.123, bf16[640,1024]{1,0:T(8,128)(2,1)} %select_dynamic-update-slice_fusion, f32[8,128,640]{1,2,0:T(8,128)} %get-tuple-element.28, f32[8,128]{1,0:T(8,128)S(1)} %get-tuple-element.27), kind=kOutput, calls=%fused_computation.92 | convolution fusion | flops 172361344 | bytes 11182080 | tf_op jit(solution)/shard_map/hqk,kd->qhd/dot_general | solution.py:68
  254.3 5.7 %fusion.105 = f32[640,1024]{1,0:T(8,128)} fusion(f32[640,1024]{1,0:T(8,128)} %fusion.107, bf16[128,8,128]{0,2,1:T(8,128)(2,1)} %bitcast.344, f32[640,128,8]{1,0,2:T(8,128)} %fusion.123, f32[8,128,640]{1,2,0:T(8,128)} %get-tuple-element.28, f32[8,128]{1,0:T(8,128)S(1)} %get-tuple-element.27), kind=kOutput, calls=%fused_computation.108 | convolution fusion | flops 172361344 | bytes 11083776 | tf_op jit(solution)/shard_map/hqk,qhd->kd/dot_general | solution.py:69
  260.0 5.8 %fusion.76 = f32[128,8,128]{2,0,1:T(8,128)} fusion(f32[640,128,8]{1,0,2:T(8,128)} %fusion.122, bf16[640,1024]{1,0:T(8,128)(2,1)} %select_dynamic-update-slice_fusion, f32[8,128,640]{1,2,0:T(8,128)} %get-tuple-element.26, f32[8,128]{1,0:T(8,128)S(1)} %get-tuple-element.25), kind=kOutput, calls=%fused_computation.95 | convolution fusion | flops 172361344 | bytes 11182080 | tf_op jit(solution)/shard_map/hqk,kd->qhd/dot_general | solution.py:68
  265.8 5.8 %fusion.103 = f32[640,1024]{1,0:T(8,128)} fusion(f32[640,1024]{1,0:T(8,128)} %fusion.105, bf16[128,8,128]{0,2,1:T(8,128)(2,1)S(1)} %bitcast.342, f32[640,128,8]{1,0,2:T(8,128)} %fusion.122, f32[8,128,640]{1,2,0:T(8,128)} %get-tuple-element.26, f32[8,128]{1,0:T(8,128)S(1)} %get-tuple-element.25), kind=kOutput, calls=%fused_computation.106 | convolution fusion | flops 172361344 | bytes 11083776 | tf_op jit(solution)/shard_map/hqk,qhd->kd/dot_general | solution.py:69
  271.7 3.1 fusion.81
  279.8 1.9 slice.115
  281.7 1.9 convert.6
  283.6 2.4 fusion.32
  286.2 5.6 %collective-permute-start.14 = (bf16[128,1024]{1,0:T(8,128)(2,1)S(1)}, bf16[128,1024]{1,0:T(8,128)(2,1)S(1)}, u32[]{:S(2)}, u32[]{:S(2)}) collective-permute-start(bf16[128,1024]{1,0:T(8,128)(2,1)S(1)} %get-tuple-element.10), channel_id=1, source_target_pairs={{0,32},{1,33},{2,34},{3,35},{4,36},{5,37},{6,38},{7,39},{8,40},{9,... | collective-permute-start | bytes 786440 | tf_op jit(solution)/shard_map/ppermute | solution.py:31
  291.9 2.5 collective-permute-start.13
  294.4 3.3 collective-permute-start.12
  297.8 2.3 fusion.36
  300.1 5.8 %collective-permute-start.11 = (bf16[128,1024]{1,0:T(8,128)(2,1)S(1)}, bf16[128,1024]{1,0:T(8,128)(2,1)S(1)}, u32[]{:S(2)}, u32[]{:S(2)}) collective-permute-start(bf16[128,1024]{1,0:T(8,128)(2,1)S(1)} %get-tuple-element.7), channel_id=1, source_target_pairs={{0,4},{1,5},{2,6},{3,7},{4,0},{5,1},{6,2},{7,3},{8,12},{9,13},{10,... | collective-permute-start | bytes 786440 | tf_op jit(solution)/shard_map/ppermute | solution.py:31
  306.0 2.6 collective-permute-start.10
  308.6 4.3 collective-permute-done.13
  312.9 1.3 collective-permute-start.9
  314.2 4.6 collective-permute-start.8
  318.8 3.0 collective-permute-done.11
  321.8 10.4 %collective-permute-done.10 = bf16[128,1024]{1,0:T(8,128)(2,1)S(1)} collective-permute-done((bf16[128,1024]{1,0:T(8,128)(2,1)S(1)}, bf16[128,1024]{1,0:T(8,128)(2,1)S(1)}, u32[]{:S(2)}, u32[]{:S(2)}) %collective-permute-start.10) | collective-permute-done | bytes 262176 | tf_op jit(solution)/shard_map/ppermute | solution.py:31
  332.9 120.4 %all-reduce.5.cloned.1.call-done = f32[128,1024]{1,0:T(8,128)} async-done(((f32[128,1024]{1,0:T(8,128)}), f32[128,1024]{1,0:T(8,128)}) %all-reduce.5.cloned.1.call-update) | async-done | bytes 524304 | tf_op jit(solution)/shard_map/psum | solution.py:158
  453.3 1.8 fusion.113
  455.8 1.3 copy.79
  (64 shorter events, 10.8 us)
Async XLA Ops:
  7.2 30.2 %copy-start.4 = (bf16[1,128,4096]{2,1,0:T(8,128)(2,1)S(1)}, bf16[1,128,4096]{2,1,0:T(8,128)(2,1)}, u32[]{:S(2)}) copy-start(bf16[1,128,4096]{2,1,0:T(8,128)(2,1)} %param.6) | copy-start | bytes 3145732
  7.2 189.3 %all-reduce.3.cloned.1.call-start = ((), (), s32[]{:S(2)}) async-start(), calls=%async_computation | async-start | bytes 524288 | tf_op jit(solution)/shard_map/psum | solution.py:25
  9.0 29.6 %copy-start.12 = (f32[1,4096]{1,0:T(1,128)S(1)}, f32[1,4096]{1,0:T(1,128)}, u32[]{:S(2)}) copy-start(f32[1,4096]{1,0:T(1,128)} %param.10) | copy-start | bytes 49156
  9.0 31.5 %collective-permute-start = (bf16[128,1024]{1,0:T(8,128)(2,1)}, bf16[128,1024]{1,0:T(8,128)(2,1)}, u32[]{:S(2)}, u32[]{:S(2)}) collective-permute-start(bf16[128,1024]{1,0:T(8,128)(2,1)} %pad_maximum_fusion), channel_id=1, source_target_pairs={{0,1},{1,2},{2,3},{3,4},{4,5},{5,6},{6,7},{7,8},{8,9},{9,10},{10,1... | collective-permute-start | bytes 786440 | tf_op jit(solution)/shard_map/ppermute | solution.py:17
  13.3 36.6 %collective-permute-start.1 = (bf16[128,1024]{1,0:T(8,128)(2,1)}, bf16[128,1024]{1,0:T(8,128)(2,1)}, u32[]{:S(2)}, u32[]{:S(2)}) collective-permute-start(bf16[128,1024]{1,0:T(8,128)(2,1)} %pad_maximum_fusion), channel_id=1, source_target_pairs={{1,0},{2,1},{3,2},{4,3},{5,4},{6,5},{7,6},{8,7},{9,8},{10,9},{11,1... | collective-permute-start | bytes 786440 | tf_op jit(solution)/shard_map/ppermute | solution.py:18
  14.6 183.5 %collective-permute-start.2 = (bf16[128,1024]{1,0:T(8,128)(2,1)}, bf16[128,1024]{1,0:T(8,128)(2,1)}, u32[]{:S(2)}, u32[]{:S(2)}) collective-permute-start(bf16[128,1024]{1,0:T(8,128)(2,1)} %pad_maximum_fusion), channel_id=1, source_target_pairs={{0,32},{1,33},{2,34},{3,35},{4,36},{5,37},{6,38},{7,39},{8,40},{9,... | collective-permute-start | bytes 786440 | tf_op jit(solution)/shard_map/ppermute | solution.py:31
  29.2 168.9 %collective-permute-start.3 = (bf16[128,1024]{1,0:T(8,128)(2,1)}, bf16[128,1024]{1,0:T(8,128)(2,1)}, u32[]{:S(2)}, u32[]{:S(2)}) collective-permute-start(bf16[128,1024]{1,0:T(8,128)(2,1)} %pad_maximum_fusion), channel_id=1, source_target_pairs={{0,16},{1,17},{2,18},{3,19},{4,20},{5,21},{6,22},{7,23},{8,24},{9,... | collective-permute-start | bytes 786440 | tf_op jit(solution)/shard_map/ppermute | solution.py:31
  32.3 165.8 %collective-permute-start.4 = (bf16[128,1024]{1,0:T(8,128)(2,1)}, bf16[128,1024]{1,0:T(8,128)(2,1)}, u32[]{:S(2)}, u32[]{:S(2)}) collective-permute-start(bf16[128,1024]{1,0:T(8,128)(2,1)} %pad_maximum_fusion), channel_id=1, source_target_pairs={{0,8},{1,9},{2,10},{3,11},{4,12},{5,13},{6,14},{7,15},{8,0},{9,1},... | collective-permute-start | bytes 786440 | tf_op jit(solution)/shard_map/ppermute | solution.py:31
  39.3 9.7 %copy-start.5 = (bf16[1,128,512]{2,1,0:T(8,128)(2,1)S(1)}, bf16[1,128,512]{2,1,0:T(8,128)(2,1)}, u32[]{:S(2)}) copy-start(bf16[1,128,512]{2,1,0:T(8,128)(2,1)} %param.9) | copy-start | bytes 393220
  39.3 9.7 %copy-start.6 = (bf16[1,128,512]{2,1,0:T(8,128)(2,1)S(1)}, bf16[1,128,512]{2,1,0:T(8,128)(2,1)}, u32[]{:S(2)}) copy-start(bf16[1,128,512]{2,1,0:T(8,128)(2,1)} %param.8) | copy-start | bytes 393220
  40.5 157.6 %collective-permute-start.5 = (bf16[128,1024]{1,0:T(8,128)(2,1)}, bf16[128,1024]{1,0:T(8,128)(2,1)}, u32[]{:S(2)}, u32[]{:S(2)}) collective-permute-start(bf16[128,1024]{1,0:T(8,128)(2,1)} %pad_maximum_fusion), channel_id=1, source_target_pairs={{0,4},{1,5},{2,6},{3,7},{4,0},{5,1},{6,2},{7,3},{8,12},{9,13},{10,... | collective-permute-start | bytes 786440 | tf_op jit(solution)/shard_map/ppermute | solution.py:31
  49.9 403.4 %all-reduce.5.cloned.1.call-start = ((), (), s32[]{:S(2)}) async-start(), calls=%async_computation.1 | async-start | bytes 1048576 | tf_op jit(solution)/shard_map/psum | solution.py:158
  50.0 148.2 %collective-permute-start.6 = (bf16[128,1024]{1,0:T(8,128)(2,1)}, bf16[128,1024]{1,0:T(8,128)(2,1)S(1)}, u32[]{:S(2)}, u32[]{:S(2)}) collective-permute-start(bf16[128,1024]{1,0:T(8,128)(2,1)} %pad_maximum_fusion), channel_id=1, source_target_pairs={{0,2},{1,3},{2,0},{3,1},{4,6},{5,7},{6,4},{7,5},{8,10},{9,11},{10,... | collective-permute-start | bytes 786440 | tf_op jit(solution)/shard_map/ppermute | solution.py:31
  200.1 3.0 copy-start.8
  217.9 3.0 copy-start.7
  271.7 3.1 copy-start.15
  274.8 1.9 copy-start.14
  276.7 1.9 copy-start.13
  286.0 11.7 %copy-start = (f32[128,8,128]{2,0,1:T(8,128)S(1)}, f32[128,8,128]{2,0,1:T(8,128)}, u32[]{:S(2)}) copy-start(f32[128,8,128]{2,0,1:T(8,128)} %fusion.67) | copy-start | bytes 1572868
  286.1 11.7 %copy-start.1 = (f32[128,8,128]{2,0,1:T(8,128)S(1)}, f32[128,8,128]{2,0,1:T(8,128)}, u32[]{:S(2)}) copy-start(f32[128,8,128]{2,0,1:T(8,128)} %fusion.70) | copy-start | bytes 1572868
  286.1 11.7 %copy-start.2 = (f32[128,8,128]{2,0,1:T(8,128)S(1)}, f32[128,8,128]{2,0,1:T(8,128)}, u32[]{:S(2)}) copy-start(f32[128,8,128]{2,0,1:T(8,128)} %fusion.73) | copy-start | bytes 1572868
  286.1 11.7 %copy-start.3 = (f32[128,8,128]{2,0,1:T(8,128)S(1)}, f32[128,8,128]{2,0,1:T(8,128)}, u32[]{:S(2)}) copy-start(f32[128,8,128]{2,0,1:T(8,128)} %fusion.76) | copy-start | bytes 1572868
  286.2 19.7 %collective-permute-start.14 = (bf16[128,1024]{1,0:T(8,128)(2,1)S(1)}, bf16[128,1024]{1,0:T(8,128)(2,1)S(1)}, u32[]{:S(2)}, u32[]{:S(2)}) collective-permute-start(bf16[128,1024]{1,0:T(8,128)(2,1)S(1)} %get-tuple-element.10), channel_id=1, source_target_pairs={{0,32},{1,33},{2,34},{3,35},{4,36},{5,37},{6,38},{7,39},{8,40},{9,... | collective-permute-start | bytes 786440 | tf_op jit(solution)/shard_map/ppermute | solution.py:31
  291.9 21.1 %collective-permute-start.13 = (bf16[128,1024]{1,0:T(8,128)(2,1)S(1)}, bf16[128,1024]{1,0:T(8,128)(2,1)S(1)}, u32[]{:S(2)}, u32[]{:S(2)}) collective-permute-start(bf16[128,1024]{1,0:T(8,128)(2,1)S(1)} %get-tuple-element.9), channel_id=1, source_target_pairs={{0,16},{1,17},{2,18},{3,19},{4,20},{5,21},{6,22},{7,23},{8,24},{9,... | collective-permute-start | bytes 786440 | tf_op jit(solution)/shard_map/ppermute | solution.py:31
  294.4 19.8 %collective-permute-start.12 = (bf16[128,1024]{1,0:T(8,128)(2,1)S(1)}, bf16[128,1024]{1,0:T(8,128)(2,1)S(1)}, u32[]{:S(2)}, u32[]{:S(2)}) collective-permute-start(bf16[128,1024]{1,0:T(8,128)(2,1)S(1)} %get-tuple-element.8), channel_id=1, source_target_pairs={{0,8},{1,9},{2,10},{3,11},{4,12},{5,13},{6,14},{7,15},{8,0},{9,1},... | collective-permute-start | bytes 786440 | tf_op jit(solution)/shard_map/ppermute | solution.py:31
  300.1 155.7 %collective-permute-start.7 = (bf16[128,4096]{0,1:T(8,128)(2,1)S(1)}, bf16[128,4096]{0,1:T(8,128)(2,1)S(1)}, u32[]{:S(2)}, u32[]{:S(2)}) collective-permute-start(bf16[128,4096]{0,1:T(8,128)(2,1)S(1)} %fusion.36), channel_id=1, source_target_pairs={{64,0},{128,64},{192,128},{256,192},{320,256},{384,320},{448,384},... | collective-permute-start | bytes 3145736 | tf_op jit(solution)/shard_map/ppermute | solution.py:37
  300.1 21.7 %collective-permute-start.11 = (bf16[128,1024]{1,0:T(8,128)(2,1)S(1)}, bf16[128,1024]{1,0:T(8,128)(2,1)S(1)}, u32[]{:S(2)}, u32[]{:S(2)}) collective-permute-start(bf16[128,1024]{1,0:T(8,128)(2,1)S(1)} %get-tuple-element.7), channel_id=1, source_target_pairs={{0,4},{1,5},{2,6},{3,7},{4,0},{5,1},{6,2},{7,3},{8,12},{9,13},{10,... | collective-permute-start | bytes 786440 | tf_op jit(solution)/shard_map/ppermute | solution.py:31
  306.0 26.2 %collective-permute-start.10 = (bf16[128,1024]{1,0:T(8,128)(2,1)S(1)}, bf16[128,1024]{1,0:T(8,128)(2,1)S(1)}, u32[]{:S(2)}, u32[]{:S(2)}) collective-permute-start(bf16[128,1024]{1,0:T(8,128)(2,1)S(1)} %get-tuple-element.11), channel_id=1, source_target_pairs={{0,2},{1,3},{2,0},{3,1},{4,6},{5,7},{6,4},{7,5},{8,10},{9,11},{10,... | collective-permute-start | bytes 786440 | tf_op jit(solution)/shard_map/ppermute | solution.py:31
  312.9 19.2 %copy-start.9 = (bf16[128,1024]{1,0:T(8,128)(2,1)}, bf16[128,1024]{1,0:T(8,128)(2,1)S(1)}, u32[]{:S(2)}) copy-start(bf16[128,1024]{1,0:T(8,128)(2,1)S(1)} %collective-permute-done.13) | copy-start | bytes 786436
  312.9 19.2 %collective-permute-start.9 = (bf16[128,1024]{1,0:T(8,128)(2,1)S(1)}, bf16[128,1024]{1,0:T(8,128)(2,1)S(1)}, u32[]{:S(2)}, u32[]{:S(2)}) collective-permute-start(bf16[128,1024]{1,0:T(8,128)(2,1)S(1)} %get-tuple-element.12), channel_id=1, source_target_pairs={{1,0},{2,1},{3,2},{4,3},{5,4},{6,5},{7,6},{8,7},{9,8},{10,9},{11,1... | collective-permute-start | bytes 786440 | tf_op jit(solution)/shard_map/ppermute | solution.py:43
  314.2 17.9 %copy-start.10 = (bf16[128,1024]{1,0:T(8,128)(2,1)}, bf16[128,1024]{1,0:T(8,128)(2,1)S(1)}, u32[]{:S(2)}) copy-start(bf16[128,1024]{1,0:T(8,128)(2,1)S(1)} %collective-permute-done.12) | copy-start | bytes 786436
  314.2 17.9 %collective-permute-start.8 = (bf16[128,1024]{1,0:T(8,128)(2,1)S(1)}, bf16[128,1024]{1,0:T(8,128)(2,1)S(1)}, u32[]{:S(2)}, u32[]{:S(2)}) collective-permute-start(bf16[128,1024]{1,0:T(8,128)(2,1)S(1)} %get-tuple-element.6), channel_id=1, source_target_pairs={{0,1},{1,2},{2,3},{3,4},{4,5},{5,6},{6,7},{7,8},{8,9},{9,10},{10,1... | collective-permute-start | bytes 786440 | tf_op jit(solution)/shard_map/ppermute | solution.py:43
  332.2 0.7 copy-start.11
Sparse Core Ops, SparseCore 0:
  50.0 146.3 all-reduce.2
  286.2 167.0 all-reduce.4
where the time goes:
time: 465 us; the launch traced here: 464 us
  waiting for transfers between devices  280 us (60%)
  matrix products  78.5 us (17%)
  starting transfers between devices  61.3 us (13%)
  between operations  15.1 us (3%)
  local copies, waits for them, and re-layouts  14.4 us (3%)
  other arithmetic  14.4 us (3%)
    psum x1, waiting for transfers between devices, broadcast(): return lax.psum(kept, axis)  142 us
    psum x1, waiting for transfers between devices, on_device(): summed = lax.psum(global_term, 'seq')  120 us
    ppermute x10, starting transfers between devices, swapped(): return lax.ppermute(value, axis, pairs)  49.8 us
    dot_general x4, matrix products, group_terms(): jnp.einsum('hqk,kd->qhd', grad_low, slot_keys, preferred_element_type=jnp...  23.3 us
    dot_general x4, matrix products, group_terms(): jnp.einsum('hqk,qhd->kd', grad_low, query_heads, preferred_element_type=j...  22.9 us
    ppermute x10, waiting for transfers between devices, swapped(): return lax.ppermute(value, axis, pairs)  17.7 us
    sub x4, matrix products, group_terms(): raised = jnp.exp(scores - row_peak)  13.7 us
    dot_general x4, matrix products, group_terms(): jnp.einsum('qhd,kd->hqk', grad_heads, slot_values, preferred_element_type...  11.7 us
  transfers between devices with their start and end apart: 17, of which 5 were waited for; matrix products, arithmetic and copies ran while one was open for 3% of the time, Pallas kernels for 0%

commit v1 on v0

v1 whole, which is shorter than its diff:
```python
import math

import jax
import jax.numpy as jnp
from jax import lax
from jax.experimental import pallas as pl
from jax.experimental.pallas import tpu as pltpu
from jax.sharding import PartitionSpec as P

MESH = pl.DeviceIdType.MESH
HD = 128
ROWS = 128
NEG = -1e30
F32 = jnp.float32
BF16 = jnp.bfloat16
SIDE = 8
DIRS = 4
PAR = (0, 1, 0, 1)


def dot(a, b, dims):
    return lax.dot_general(a, b, (dims, ((), ())), preferred_element_type=F32)


def kernel(
    heads,
    groups,
    gain,
    rand,
    stream,
    cotangent,
    keys,
    values,
    stream_out,
    key_out,
    value_out,
    hidden,
    upstream,
    queries,
    grad_query,
    handed,
    blocks,
    corner,
    halo,
    slot_keys,
    slot_values,
    terms,
    far_out,
    far_in,
    far_in2,
    mid_out,
    mid_in,
    near_out,
    near_in,
    edge_out,
    edge_in,
    global_out,
    global_in,
    column_sum,
    column_out,
    row_in,
    row_out,
    last_in,
    local_sem,
    kv_send,
    kv_recv,
    halo_send,
    halo_recv,
    corner_send,
    corner_recv,
    ret_send,
    ret_recv,
    edge_sem,
    global_send,
    global_recv,
    row_send,
    row_recv,
    last_send,
    last_recv,
    handed_sem,
):
    device = lax.axis_index("seq")
    section = lax.axis_index("section")
    sections = lax.axis_size("section")
    z, y = device // SIDE, device % SIDE
    wanted = rand[0, 0]
    pieces = 2 * groups
    per_group = heads // groups
    factor = HD ** (-0.5)

    def at(direction, distance):
        if direction == 0:
            return z * SIDE + (y + distance) % SIDE
        if direction == 1:
            return z * SIDE + (y + SIDE - distance) % SIDE
        if direction == 2:
            return ((z + distance) % SIDE) * SIDE + y
        return ((z + SIDE - distance) % SIDE) * SIDE + y

    def remote(src, dst, send, recv, to):
        return pltpu.make_async_remote_copy(
            src_ref=src,
            dst_ref=dst,
            send_sem=send,
            recv_sem=recv,
            device_id={"seq": to},
            device_id_type=MESH,
        )

    own = []
    for g in range(groups):
        columns = pl.ds(g * HD, HD)
        own.append(pltpu.make_async_copy(keys.at[0, :, columns], blocks.at[0, 2 * g], local_sem.at[2 * g]))
        own.append(
            pltpu.make_async_copy(values.at[0, :, columns], blocks.at[0, 2 * g + 1], local_sem.at[2 * g + 1])
        )
    for copy in own:
        copy.start()
    load_hidden = pltpu.make_async_copy(stream.at[0], hidden, local_sem.at[pieces])
    load_upstream = pltpu.make_async_copy(cotangent.at[0], upstream, local_sem.at[pieces + 1])
    load_hidden.start()
    load_upstream.start()

    barrier = pltpu.get_barrier_semaphore()

    def greet(k, carry):
        pl.semaphore_signal(barrier, inc=1, device_id={"seq": at(0, k)}, device_id_type=MESH)
        pl.semaphore_signal(barrier, inc=1, device_id={"seq": at(2, k)}, device_id_type=MESH)
        return carry

    lax.fori_loop(1, SIDE, greet, 0)
    before = (section + sections - 1) % sections
    after = (section + 1) % sections
    pl.semaphore_signal(barrier, inc=1, device_id={"section": before}, device_id_type=MESH)
    pl.semaphore_signal(barrier, inc=1, device_id={"section": after}, device_id_type=MESH)
    for copy in own:
        copy.wait()
    pl.semaphore_wait(barrier, 2 * (SIDE - 1) + 2)

    def corner_copy(stage, piece, to, index):
        src = blocks.at[0, piece] if stage == 0 else corner.at[piece]
        return remote(src, corner.at[piece], corner_send.at[stage, index], corner_recv.at[piece], to)

    @pl.when(device == 0)
    def _():
        corner[0] = blocks[0, 0]

        def scatter(p, carry):
            corner_copy(0, p, p * SIDE, p).start()
            return carry

        lax.fori_loop(1, SIDE, scatter, 0)

    def slot(direction, step):
        return (step, SIDE - step, SIDE + step, 2 * SIDE - step)[direction]

    def kv(direction, step, g):
        part = pl.ds(2 * g, 2) if step <= 2 else pl.ds(2 * g + PAR[direction], 1)
        src = blocks.at[0 if step == 1 else slot(direction, step - 1), part]
        return remote(
            src,
            blocks.at[slot(direction, step), part],
            kv_send.at[direction, step - 1, g],
            kv_recv.at[direction, step - 1, g],
            at(direction, 1),
        )

    def first(g, carry):
        for direction in range(DIRS):
            kv(direction, 1, g).start()
        return carry

    lax.fori_loop(0, groups, first, 0)

    load_hidden.wait()

    def square(h, total):
        x = hidden[:, pl.ds(pl.multiple_of(h * HD, HD), HD)].astype(F32)
        return total + x * x

    squares = lax.fori_loop(0, heads, square, jnp.zeros((ROWS, HD), F32))
    inverse = lax.rsqrt(jnp.sum(squares, axis=1, keepdims=True) / (heads * HD) + 1e-05)

    def query(h, carry):
        columns = pl.ds(pl.multiple_of(h * HD, HD), HD)
        normed = hidden[:, columns].astype(F32) * inverse
        queries[:, columns] = (normed * gain[:, columns]).astype(BF16)
        return carry

    lax.fori_loop(0, heads, query, 0)

    def halo_copy(g, source, to):
        part = pl.ds(2 * g, 2)
        return remote(blocks.at[source, part], halo.at[part], halo_send.at[g], halo_recv.at[g], to)

    def second(g, carry):
        for direction in (2, 3, 0, 1):
            kv(direction, 1, g).wait_recv()
            kv(direction, 2, g).start()

        @pl.when(y == SIDE - 1)
        def _():
            halo_copy(g, SIDE + 1, z * SIDE).start()

        @pl.when(y == 0)
        def _():
            halo_copy(g, 2 * SIDE - 1, z * SIDE + SIDE - 1).start()

        return carry

    lax.fori_loop(0, groups, second, 0)

    @pl.when(y == 0)
    def _():
        @pl.when(z != 0)
        def _():
            corner_copy(1, z, device, 0).wait_recv()

        def spread(k, carry):
            corner_copy(1, z, at(0, k), k).start()
            return carry

        lax.fori_loop(1, SIDE, spread, 0)

    def onward(step):
        def body(g, carry):
            for direction in range(DIRS):
                kv(direction, step - 1, g).wait_recv()
                kv(direction, step, g).start()
            return carry

        lax.fori_loop(0, groups, body, 0)

    onward(3)

    @pl.when(y != 0)
    def _():
        corner_copy(2, z, device, 0).wait_recv()

    def column(k, carry):
        corner_copy(2, z, at(2, k), k).start()
        return carry

    lax.fori_loop(1, SIDE, column, 0)

    onward(4)

    def collect(g, carry):
        for direction in range(DIRS):
            kv(direction, 4, g).wait_recv()

        @pl.when((y == 0) | (y == SIDE - 1))
        def _():
            halo_copy(g, 0, device).wait_recv()

        return carry

    lax.fori_loop(0, groups, collect, 0)

    def collect_corner(k, carry):
        corner_copy(2, (z + k) % SIDE, device, 0).wait_recv()
        return carry

    lax.fori_loop(1, SIDE, collect_corner, 0)

    wanted_z, wanted_y = wanted // SIDE, wanted % SIDE
    picked = jnp.where(
        wanted_z == z, (y + SIDE - wanted_y) % SIDE, SIDE + (z + SIDE - wanted_z) % SIDE
    )

    def assemble(p, carry):
        for kv_index, target in ((0, slot_keys), (1, slot_values)):
            piece = 2 * p + kv_index
            target[p, pl.ds(0, ROWS)] = jnp.where(y == 0, halo[piece], blocks[1, piece])
            target[p, pl.ds(ROWS, ROWS)] = blocks[0, piece]
            target[p, pl.ds(2 * ROWS, ROWS)] = jnp.where(
                y == SIDE - 1, halo[piece], blocks[SIDE - 1, piece]
            )
            target[p, pl.ds(3 * ROWS, ROWS)] = corner[piece]
            target[p, pl.ds(4 * ROWS, ROWS)] = blocks[picked, piece]
        return carry

    lax.fori_loop(0, groups, assemble, 0)
    terms[...] = jnp.zeros_like(terms)

    load_upstream.wait()

    no_before = jnp.where(device == 0, NEG, 0.0).astype(F32)
    no_after = jnp.where(device == SIDE * SIDE - 1, NEG, 0.0).astype(F32)
    bias = (no_before, None, no_after, no_before, None)
    scale = factor * math.log2(math.e)

    def unit(u, carry):
        g = u // (per_group // 2)
        left = pl.ds(pl.multiple_of(2 * u * HD, HD), HD)
        right = pl.ds(pl.multiple_of(2 * u * HD + HD, HD), HD)
        q = jnp.concatenate([queries[:, left], queries[:, right]], axis=0)
        do = jnp.concatenate([upstream[:, left], upstream[:, right]], axis=0)
        k, v = slot_keys[g], slot_values[g]
        raw = dot(k, q, ((1,), (1,)))
        grad_weights = dot(v, do, ((1,), (1,)))
        scores = []
        for i in range(5):
            part = raw[i * ROWS : (i + 1) * ROWS] * scale
            scores.append(part if bias[i] is None else part + bias[i])
        scores = jnp.concatenate(scores, axis=0)
        peak = jnp.max(scores, axis=0, keepdims=True)
        raised = jnp.exp2(scores - peak)
        weights = raised * (1.0 / jnp.sum(raised, axis=0, keepdims=True))
        row_dot = jnp.sum(weights * grad_weights, axis=0, keepdims=True)
        grad_low = (weights * (grad_weights - row_dot) * factor).astype(BF16)
        weights_low = weights.astype(BF16)
        terms[2 * g] += dot(grad_low, q, ((1,), (0,)))
        terms[2 * g + 1] += dot(weights_low, do, ((1,), (0,)))
        back = dot(grad_low, k, ((0,), (0,)))
        grad_query[:, left] = back[:ROWS]
        grad_query[:, right] = back[ROWS:]
        return carry

    lax.fori_loop(0, heads // 2, unit, 0)

    def mark(to):
        return jnp.where(wanted == to, 1.0, 0.0).astype(F32)

    before_rows, own_rows, after_rows, global_rows, random_rows = (
        pl.ds(i * ROWS, ROWS) for i in range(5)
    )

    def ret(direction, step, g):
        pair = {4: (far_out, far_in), 3: (far_in, far_in2), 2: (mid_out, mid_in), 1: (near_out, near_in)}
        src, dst = pair[step]
        return remote(
            src.at[direction, g],
            dst.at[direction, g],
            ret_send.at[direction, step - 1, g],
            ret_recv.at[direction, step - 1, g],
            at(direction, 1),
        )

    def global_copy(piece, index):
        return remote(
            global_out.at[piece],
            global_in.at[z],
            global_send.at[index],
            global_recv.at[z],
            piece * SIDE + y,
        )

    def edge_copy(to):
        return remote(edge_out, edge_in, edge_sem.at[0], edge_sem.at[1], to)

    def to_bf16(p, carry):
        global_out[p] = terms[p, global_rows].astype(BF16)
        return carry

    lax.fori_loop(0, pieces, to_bf16, 0)

    def send_global(k, carry):
        global_copy((z + k) % SIDE, k).start()
        return carry

    lax.fori_loop(1, SIDE, send_global, 0)

    def send_far(g, carry):
        for direction in range(DIRS):
            random = terms[2 * g + PAR[direction], random_rows]
            far_out[direction, g] = (random * mark(at(direction, 4))).astype(BF16)
            ret(direction, 4, g).start()
        return carry

    lax.fori_loop(0, groups, send_far, 0)

    @pl.when(y == SIDE - 1)
    def _():
        def fill(p, carry):
            edge_out[p] = terms[p, after_rows].astype(BF16)
            return carry

        lax.fori_loop(0, pieces, fill, 0)
        edge_copy(at(2, 1)).start()

    @pl.when(y == 0)
    def _():
        def fill(p, carry):
            edge_out[p] = terms[p, before_rows].astype(BF16)
            return carry

        lax.fori_loop(0, pieces, fill, 0)
        edge_copy(at(3, 1)).start()

    def product(h, total):
        columns = pl.ds(pl.multiple_of(h * HD, HD), HD)
        normed = hidden[:, columns].astype(F32) * inverse
        return total + grad_query[:, columns] * gain[:, columns] * normed

    products = lax.fori_loop(0, heads, product, jnp.zeros((ROWS, HD), F32))
    mean = jnp.sum(products, axis=1, keepdims=True) / (heads * HD)

    def hand(h, carry):
        columns = pl.ds(pl.multiple_of(h * HD, HD), HD)
        normed = hidden[:, columns].astype(F32) * inverse
        grad_norm = grad_query[:, columns] * gain[:, columns]
        grad = inverse * (grad_norm - normed * mean)
        handed[:, columns] = (upstream[:, columns].astype(F32) + grad).astype(BF16)
        return carry

    lax.fori_loop(0, heads, hand, 0)
    hand_over = pltpu.make_async_remote_copy(
        src_ref=handed,
        dst_ref=stream_out.at[0],
        send_sem=handed_sem.at[0],
        recv_sem=handed_sem.at[1],
        device_id={"section": before},
        device_id_type=MESH,
    )
    hand_over.start()

    def pass_far(g, carry):
        for direction in range(DIRS):
            ret(direction, 4, g).wait_recv()
            ret(direction, 3, g).start()
        return carry

    lax.fori_loop(0, groups, pass_far, 0)

    def add_column(k, total):
        source = (z + k) % SIDE
        remote(
            global_out.at[0], global_in.at[source], global_send.at[0], global_recv.at[source], device
        ).wait_recv()
        return total + global_in[source].astype(F32)

    column_sum[...] = lax.fori_loop(1, SIDE, add_column, terms[z, global_rows])

    def row_copy(source, to):
        return remote(column_out, row_in.at[source], row_send.at[0], row_recv.at[source], to)

    @pl.when(y != 0)
    def _():
        column_out[...] = column_sum[...].astype(BF16)
        row_copy(y, z * SIDE).start()

    def send_mid(g, carry):
        for direction in range(DIRS):
            ret(direction, 3, g).wait_recv()
            here = mark(at(direction, 2))
            half = PAR[direction]
            mid_out[direction, g, half] = (
                terms[2 * g + half, random_rows] * here + far_in2[direction, g].astype(F32)
            ).astype(BF16)
            mid_out[direction, g, 1 - half] = (terms[2 * g + 1 - half, random_rows] * here).astype(BF16)
            ret(direction, 2, g).start()
        return carry

    lax.fori_loop(0, groups, send_mid, 0)

    def last_copy(source, to):
        return remote(row_out, last_in.at[source], last_send.at[0], last_recv.at[source], to)

    @pl.when(y == 0)
    def _():
        def add_row(k, total):
            row_copy(k, device).wait_recv()
            return total + row_in[k].astype(F32)

        column_sum[...] = lax.fori_loop(1, SIDE, add_row, column_sum[...])

        @pl.when(z != 0)
        def _():
            row_out[...] = column_sum[...].astype(BF16)
            last_copy(z, 0).start()

    @pl.when((y == 0) | (y == SIDE - 1))
    def _():
        edge_copy(device).wait_recv()

    def send_near(g, carry):
        for direction in range(DIRS):
            ret(direction, 2, g).wait_recv()
            for kv_index in range(2):
                p = 2 * g + kv_index
                passed = mid_in[direction, g, kv_index].astype(F32)
                if direction == 0:
                    added = jnp.where(
                        y == SIDE - 1,
                        edge_in[p].astype(F32),
                        terms[p, after_rows].astype(BF16).astype(F32),
                    )
                elif direction == 1:
                    added = jnp.where(
                        y == 0,
                        edge_in[p].astype(F32),
                        terms[p, before_rows].astype(BF16).astype(F32),
                    )
                else:
                    added = terms[p, random_rows] * mark(at(direction, 1))
                near_out[direction, g, kv_index] = (passed + added).astype(BF16)
            ret(direction, 1, g).start()
        return carry

    lax.fori_loop(0, groups, send_near, 0)

    @pl.when(device == 0)
    def _():
        def take(p, carry):
            last_copy(p, device).wait_recv()
            terms[p, own_rows] += last_in[p].astype(F32)
            return carry

        lax.fori_loop(1, SIDE, take, 0)
        terms[0, own_rows] += column_sum[...]

    for g in range(groups):
        for direction in range(DIRS):
            ret(direction, 1, g).wait_recv()
        for kv_index, out in ((0, key_out), (1, value_out)):
            total = terms[2 * g + kv_index, own_rows]
            for direction in range(DIRS):
                total = total + near_in[direction, g, kv_index].astype(F32)
            out[0, :, pl.ds(g * HD, HD)] = total.astype(BF16)

    def sent(g, carry):
        for direction in range(DIRS):
            for step in (1, 2, 3, 4):
                kv(direction, step, g).wait_send()
                ret(direction, step, g).wait_send()

        @pl.when((y == 0) | (y == SIDE - 1))
        def _():
            halo_copy(g, 0, device).wait_send()

        return carry

    lax.fori_loop(0, groups, sent, 0)

    def sent_pieces(k, carry):
        corner_copy(2, 0, device, k).wait_send()
        global_copy(0, k).wait_send()
        return carry

    lax.fori_loop(1, SIDE, sent_pieces, 0)

    @pl.when(y == 0)
    def _():
        def sent_rows(k, carry):
            corner_copy(1, 0, device, k).wait_send()
            return carry

        lax.fori_loop(1, SIDE, sent_rows, 0)

        @pl.when(z == 0)
        def _():
            def sent_corner(k, carry):
                corner_copy(0, 0, device, k).wait_send()
                return carry

            lax.fori_loop(1, SIDE, sent_corner, 0)

        @pl.when(z != 0)
        def _():
            last_copy(z, 0).wait_send()

    @pl.when(y != 0)
    def _():
        row_copy(y, z * SIDE).wait_send()

    @pl.when((y == 0) | (y == SIDE - 1))
    def _():
        edge_copy(device).wait_send()

    hand_over.wait()


def solution(mesh):
    def on_device(stream, cotangent, keys, values, gain, rand_blocks):
        heads = stream.shape[2] // HD
        groups = keys.shape[2] // HD
        pieces = 2 * groups
        block = (ROWS, HD)
        vmem = pl.BlockSpec(memory_space=pltpu.VMEM)
        hbm = pl.BlockSpec(memory_space=pl.ANY)
        dma = pltpu.SemaphoreType.DMA

        def bf16(*shape):
            return pltpu.VMEM(shape, BF16)

        def f32(*shape):
            return pltpu.VMEM(shape, F32)

        def body(*refs):
            kernel(heads, groups, *refs)

        return pl.pallas_call(
            body,
            name="relay",
            out_shape=(
                jax.ShapeDtypeStruct(stream.shape, BF16),
                jax.ShapeDtypeStruct(keys.shape, BF16),
                jax.ShapeDtypeStruct(values.shape, BF16),
            ),
            in_specs=[vmem, pl.BlockSpec(memory_space=pltpu.SMEM), hbm, hbm, hbm, hbm],
            out_specs=(hbm, vmem, vmem),
            scratch_shapes=[
                bf16(ROWS, heads * HD),
                bf16(ROWS, heads * HD),
                bf16(ROWS, heads * HD),
                f32(ROWS, heads * HD),
                bf16(ROWS, heads * HD),
                bf16(2 * SIDE, pieces, *block),
                bf16(pieces, *block),
                bf16(pieces, *block),
                bf16(groups, 5 * ROWS, HD),
                bf16(groups, 5 * ROWS, HD),
                f32(pieces, 5 * ROWS, HD),
                bf16(DIRS, groups, *block),
                bf16(DIRS, groups, *block),
                bf16(DIRS, groups, *block),
                bf16(DIRS, groups, 2, *block),
                bf16(DIRS, groups, 2, *block),
                bf16(DIRS, groups, 2, *block),
                bf16(DIRS, groups, 2, *block),
                bf16(pieces, *block),
                bf16(pieces, *block),
                bf16(pieces, *block),
                bf16(SIDE, *block),
                f32(*block),
                bf16(*block),
                bf16(SIDE, *block),
                bf16(*block),
                bf16(SIDE, *block),
                dma((pieces + 2,)),
                dma((DIRS, 4, groups)),
                dma((DIRS, 4, groups)),
                dma((groups,)),
                dma((groups,)),
                dma((3, SIDE)),
                dma((pieces,)),
                dma((DIRS, 4, groups)),
                dma((DIRS, 4, groups)),
                dma((2,)),
                dma((SIDE,)),
                dma((SIDE,)),
                dma((1,)),
                dma((SIDE,)),
                dma((1,)),
                dma((SIDE,)),
                dma((2,)),
            ],
            compiler_params=pltpu.CompilerParams(
                collective_id=0, has_side_effects=True, vmem_limit_bytes=48 * 1024 * 1024
            ),
        )(gain, rand_blocks, stream, cotangent, keys, values)

    return jax.shard_map(
        on_device,
        mesh=mesh,
        in_specs=(
            P("section", "seq", None),
            P("section", "seq", None),
            P("section", "seq", None),
            P("section", "seq", None),
            P("section", None),
            P("seq", None),
        ),
        out_specs=(P("section", "seq", None), P("section", "seq", None), P("section", "seq", None)),
        check_vma=False,
    )
```

time: 465 us -> 100 us (0.22)
  waiting for transfers between devices: 280 us -> 0 us
  Pallas kernels: 0 us -> 91.5 us
  matrix products: 78.5 us -> 0 us
  starting transfers between devices: 61.3 us -> 0 us
  other arithmetic: 14.4 us -> 0 us
  between operations: 15.1 us -> 1.3 us
  local copies, waits for them, and re-layouts: 14.4 us -> 7.25 us
    psum x2 -> x0, waiting for transfers between devices: 262 us -> none  [the longest x1 142 us: broadcast(): return lax.psum(kept, axis)]
    pallas_call x0 -> x1, Pallas kernels: none -> 91.5 us  [on_device(): pl.pallas_call(body, name='relay', out_shape=(jax.ShapeDtypeStruct(stream...]
    dot_general x16 -> x0, matrix products: 64.8 us -> none  [the longest x4 23.3 us: group_terms(): jnp.einsum('hqk,kd->qhd', grad_low, slot_keys, preferred_element_type=jnp...]
    ppermute x15 -> x0, starting transfers between devices: 61.2 us -> none  [the longest x10 49.8 us: swapped(): return lax.ppermute(value, axis, pairs)]
    ppermute x15 -> x0, waiting for transfers between devices: 17.7 us -> none  [the longest x10 17.7 us: swapped(): return lax.ppermute(value, axis, pairs)]
    sub x4 -> x0, matrix products: 13.7 us -> none  [group_terms(): raised = jnp.exp(scores - row_peak)]
    convert_element_type x3 -> x0, other arithmetic: 4.8 us -> none  [the longest x1 2.31 us: on_device(): handed = (upstream.astype(jnp.float32) + grad_hidden).astype(jnp.bfloat16)]
    unnamed x38 -> x13, local copies, waits for them, and re-layouts: 10.5 us -> 7.25 us
  transfers between devices with their start and end apart: 17 -> 0, of which waited for: 5 -> 0; matrix products, arithmetic and copies ran while one was open for 3% -> 0% of each run, Pallas kernels for 0% -> 0%
where the time goes in v1:
time: 100 us
  Pallas kernels  91.5 us (92%)
  local copies, waits for them, and re-layouts  7.25 us (7%)
  between operations  1.3 us (1%)
    pallas_call x1, Pallas kernels, on_device(): pl.pallas_call(body, name='relay', out_shape=(jax.ShapeDtypeStruct(stream...  91.5 us
    unnamed x13, local copies, waits for them, and re-layouts  7.25 us

profile of v1, /device:TPU:6, one launch (start us, length us, event | category | flops | bytes accessed | tf_op | source)
XLA Modules:
  0.0 100.1 jit_solution(14077344696054033237)
XLA Ops:
  1.3 0.0 copy-start
  1.3 1.2 %copy-done = bf16[1,128,4096]{2,1,0:T(8,128)(2,1)S(1)} copy-done((bf16[1,128,4096]{2,1,0:T(8,128)(2,1)S(1)}, bf16[1,128,4096]{2,1,0:T(8,128)(2,1)}, u32[]{:S(2)}) %copy-start) | copy-done | bytes 1048600
  2.5 0.0 copy-start.1
  2.5 1.2 %copy-done.1 = bf16[1,128,4096]{2,1,0:T(8,128)(2,1)S(1)} copy-done((bf16[1,128,4096]{2,1,0:T(8,128)(2,1)S(1)}, bf16[1,128,4096]{2,1,0:T(8,128)(2,1)}, u32[]{:S(2)}) %copy-start.1) | copy-done | bytes 1048600
  3.7 0.0 copy-start.2
  3.7 0.9 copy-done.2
  4.6 0.0 copy-start.3
  4.6 0.9 copy-done.3
  5.5 0.0 copy-start.4
  5.5 0.7 copy-done.4
  6.3 91.5 %relay.1 = (bf16[1,128,4096]{2,1,0:T(8,128)(2,1)S(1)}, bf16[1,128,512]{2,1,0:T(8,128)(2,1)S(1)}, bf16[1,128,512]{2,1,0:T(8,128)(2,1)S(1)}) custom-call(f32[1,4096]{1,0:T(1,128)S(1)} %copy-done.4, s32[1,1]{1,0:T(1,128)S(6)} %copy.12.refs_1_, bf16[1,128,4096]{2,1,0:T(8,128)(2,1)S(1)} %copy-done, bf16[1,128,4096]{2,1,0:T(8,128)(2,1)S(1)} %copy-done.1, ...), custom_call_target="tpu_custom_call" | custom-call | tf_op jit(solution)/shard_map/relay/pallas_call | solution.py:593
  97.8 1.0 copy.13
  98.8 0.7 copy.14
  99.4 0.7 copy.15
Async XLA Ops:
  1.3 1.2 %copy-start = (bf16[1,128,4096]{2,1,0:T(8,128)(2,1)S(1)}, bf16[1,128,4096]{2,1,0:T(8,128)(2,1)}, u32[]{:S(2)}) copy-start(bf16[1,128,4096]{2,1,0:T(8,128)(2,1)} %refs_2_.1) | copy-start | bytes 3145732
  2.5 1.2 %copy-start.1 = (bf16[1,128,4096]{2,1,0:T(8,128)(2,1)S(1)}, bf16[1,128,4096]{2,1,0:T(8,128)(2,1)}, u32[]{:S(2)}) copy-start(bf16[1,128,4096]{2,1,0:T(8,128)(2,1)} %refs_3_.1) | copy-start | bytes 3145732
  3.7 0.9 copy-start.2
  4.6 0.9 copy-start.3
  5.5 0.7 copy-start.4

commit v2 on v1

v2 whole, which is shorter than its diff:
```python
import math

import jax
import jax.numpy as jnp
from jax import lax
from jax.experimental import pallas as pl
from jax.experimental.pallas import tpu as pltpu
from jax.sharding import PartitionSpec as P

MESH = pl.DeviceIdType.MESH
HD = 128
ROWS = 128
HALF = ROWS // 2
NEG = -1e30
F32 = jnp.float32
BF16 = jnp.bfloat16
SIDE = 8
DIRS = 4
PAR = (0, 1, 0, 1)


def dot(a, b, dims):
    return lax.dot_general(a, b, (dims, ((), ())), preferred_element_type=F32)


def kernel(
    heads,
    groups,
    rand,
    gain_in,
    stream,
    cotangent,
    keys,
    values,
    stream_out,
    key_out,
    value_out,
    gain,
    hidden,
    upstream,
    queries,
    grad_query,
    handed,
    products,
    blocks,
    corner,
    halo,
    slot_keys,
    slot_values,
    terms,
    far_out,
    far_in,
    far_in2,
    mid_out,
    mid_in,
    near_out,
    near_in,
    edge_out,
    edge_in,
    global_out,
    global_in,
    line_sum,
    line_out,
    cross_in,
    cross_out,
    last_in,
    local_sem,
    kv_send,
    kv_recv,
    halo_send,
    halo_recv,
    corner_send,
    corner_recv,
    ret_send,
    ret_recv,
    edge_send,
    edge_recv,
    global_send,
    global_recv,
    cross_send,
    cross_recv,
    last_send,
    last_recv,
    handed_send,
    handed_recv,
):
    device = lax.axis_index("seq")
    section = lax.axis_index("section")
    sections = lax.axis_size("section")
    z, y = device // SIDE, device % SIDE
    wanted = rand[0, 0]
    pieces = 2 * groups
    per_group = heads // groups
    factor = HD ** (-0.5)
    edge = (y == 0) | (y == SIDE - 1)

    def at(direction, distance):
        if direction == 0:
            return z * SIDE + (y + distance) % SIDE
        if direction == 1:
            return z * SIDE + (y + SIDE - distance) % SIDE
        if direction == 2:
            return ((z + distance) % SIDE) * SIDE + y
        return ((z + SIDE - distance) % SIDE) * SIDE + y

    def remote(src, dst, send, recv, to):
        return pltpu.make_async_remote_copy(
            src_ref=src,
            dst_ref=dst,
            send_sem=send,
            recv_sem=recv,
            device_id={"seq": to},
            device_id_type=MESH,
        )

    def each(low, high, body):
        def step(i, carry):
            body(i)
            return carry

        lax.fori_loop(low, high, step, 0)

    own = []
    for g in range(groups):
        columns = pl.ds(g * HD, HD)
        own.append(pltpu.make_async_copy(keys.at[0, :, columns], blocks.at[0, 2 * g], local_sem.at[2 * g]))
        own.append(
            pltpu.make_async_copy(values.at[0, :, columns], blocks.at[0, 2 * g + 1], local_sem.at[2 * g + 1])
        )
    for copy in own:
        copy.start()
    load_gain = pltpu.make_async_copy(gain_in, gain, local_sem.at[pieces])
    load_hidden = pltpu.make_async_copy(stream.at[0], hidden, local_sem.at[pieces + 1])
    load_upstream = pltpu.make_async_copy(cotangent.at[0], upstream, local_sem.at[pieces + 2])
    load_gain.start()
    load_hidden.start()
    load_upstream.start()

    barrier = pltpu.get_barrier_semaphore()

    def greet(k):
        pl.semaphore_signal(barrier, inc=1, device_id={"seq": at(0, k)}, device_id_type=MESH)
        pl.semaphore_signal(barrier, inc=1, device_id={"seq": at(2, k)}, device_id_type=MESH)

    each(1, SIDE, greet)
    before = (section + sections - 1) % sections
    after = (section + 1) % sections
    pl.semaphore_signal(barrier, inc=1, device_id={"section": before}, device_id_type=MESH)
    pl.semaphore_signal(barrier, inc=1, device_id={"section": after}, device_id_type=MESH)
    for copy in own:
        copy.wait()
    pl.semaphore_wait(barrier, 2 * (SIDE - 1) + 2)

    line = (z, y)
    cross = (y, z)
    along = (2, 0)
    across = (0, 2)

    def corner_copy(stage, half, i, to, index):
        if stage == 0:
            src = blocks.at[0, 2 * (i // 2) + half, pl.ds((i % 2) * HALF, HALF)]
        else:
            src = corner.at[half, i]
        return remote(
            src, corner.at[half, i], corner_send.at[stage, half, index], corner_recv.at[half, i], to
        )

    @pl.when(device == 0)
    def _():
        corner[0, 0] = blocks[0, 0, :HALF]
        corner[1, 0] = blocks[0, 1, :HALF]

        def scatter(i):
            for half in range(2):
                corner_copy(0, half, i, at(along[half], i), i).start()

        each(1, SIDE, scatter)

    def slot(direction, step):
        return (step, SIDE - step, SIDE + step, 2 * SIDE - step)[direction]

    def kv(direction, step, g):
        part = pl.ds(2 * g, 2) if step <= 2 else pl.ds(2 * g + PAR[direction], 1)
        src = blocks.at[0 if step == 1 else slot(direction, step - 1), part]
        return remote(
            src,
            blocks.at[slot(direction, step), part],
            kv_send.at[direction, step - 1, g],
            kv_recv.at[direction, step - 1, g],
            at(direction, 1),
        )

    def halo_copy(g, source, to):
        part = pl.ds(2 * g, 2)
        return remote(blocks.at[source, part], halo.at[part], halo_send.at[g], halo_recv.at[g], to)

    def forward(step, g):
        for direction in range(DIRS):
            if step > 1:
                kv(direction, step - 1, g).wait_recv()
            kv(direction, step, g).start()
        if step == 2:

            @pl.when(y == SIDE - 1)
            def _():
                halo_copy(g, SIDE + 1, z * SIDE).start()

            @pl.when(y == 0)
            def _():
                halo_copy(g, 2 * SIDE - 1, z * SIDE + SIDE - 1).start()

    forward(1, 0)
    forward(1, 1)

    load_hidden.wait()

    def square(h, total):
        x = hidden[:, pl.ds(pl.multiple_of(h * HD, HD), HD)].astype(F32)
        return total + x * x

    squares = lax.fori_loop(0, heads, square, jnp.zeros((ROWS, HD), F32))
    inverse = lax.rsqrt(jnp.sum(squares, axis=1, keepdims=True) / (heads * HD) + 1e-05)
    load_gain.wait()

    def query(h):
        columns = pl.ds(pl.multiple_of(h * HD, HD), HD)
        normed = hidden[:, columns].astype(F32) * inverse
        queries[:, columns] = (normed * gain[:, columns]).astype(BF16)

    each(0, heads, query)
    products[...] = jnp.zeros_like(products)

    forward(2, 0)
    forward(1, 2)
    forward(2, 1)

    for half in range(2):

        @pl.when(cross[half] == 0)
        def _():
            @pl.when(line[half] != 0)
            def _():
                corner_copy(1, half, line[half], device, 0).wait_recv()

            def spread(k):
                corner_copy(1, half, line[half], at(across[half], k), k).start()

            each(1, SIDE, spread)

    forward(3, 0)
    forward(1, 3)
    forward(2, 2)
    forward(4, 0)
    forward(3, 1)

    for half in range(2):

        @pl.when(cross[half] != 0)
        def _():
            corner_copy(2, half, line[half], device, 0).wait_recv()

    def over_lines(k):
        for half in range(2):
            corner_copy(2, half, line[half], at(along[half], k), k).start()

    each(1, SIDE, over_lines)
    forward(2, 3)
    forward(3, 2)
    load_upstream.wait()

    def collect(g):
        for direction in range(DIRS):
            kv(direction, 4, g).wait_recv()

        @pl.when(edge)
        def _():
            halo_copy(g, 0, device).wait_recv()

        for half in range(2):
            for i in range(2):

                @pl.when(line[half] != 2 * g + i)
                def _():
                    corner_copy(2, half, 2 * g + i, device, 0).wait_recv()

    partners = (
        (y + 2 - 4 * ((y // 2) % 2), None),
        ((y + 4) % SIDE, None),
        (None, z + 1 - 2 * (z % 2)),
        (None, z + 2 - 4 * ((z // 2) % 2)),
        (None, (z + 4) % SIDE),
    )

    def assemble(g):
        for half, target in ((0, slot_keys), (1, slot_values)):
            piece = 2 * g + half
            target[g, pl.ds(0, ROWS)] = jnp.where(y == 0, halo[piece], blocks[1, piece])
            target[g, pl.ds(ROWS, ROWS)] = blocks[0, piece]
            target[g, pl.ds(2 * ROWS, ROWS)] = jnp.where(
                y == SIDE - 1, halo[piece], blocks[SIDE - 1, piece]
            )
            for i in range(2):
                target[g, pl.ds(3 * ROWS + i * HALF, HALF)] = corner[half, 2 * g + i]
            picked = None
            for to_y, to_z in partners:
                if to_z is None:
                    name, place = z * SIDE + to_y, (y + SIDE - to_y) % SIDE
                else:
                    name, place = to_z * SIDE + y, SIDE + (z + SIDE - to_z) % SIDE
                block = blocks[place, piece]
                picked = block if picked is None else jnp.where(wanted == name, block, picked)
            target[g, pl.ds(4 * ROWS, ROWS)] = picked

    no_before = jnp.where(device == 0, NEG, 0.0).astype(F32)
    no_after = jnp.where(device == SIDE * SIDE - 1, NEG, 0.0).astype(F32)
    bias = (no_before, None, no_after, no_before, None)
    scale = factor * math.log2(math.e)

    def unit(g, first_head, count, fresh):
        columns = [pl.ds(pl.multiple_of((first_head + i) * HD, HD), HD) for i in range(count)]
        q = jnp.concatenate([queries[:, c] for c in columns], axis=0)
        do = jnp.concatenate([upstream[:, c] for c in columns], axis=0)
        k, v = slot_keys[g], slot_values[g]
        raw = dot(k, q, ((1,), (1,)))
        grad_weights = dot(v, do, ((1,), (1,)))
        scores = []
        for i in range(5):
            part = raw[i * ROWS : (i + 1) * ROWS] * scale
            scores.append(part if bias[i] is None else part + bias[i])
        scores = jnp.concatenate(scores, axis=0)
        peak = jnp.max(scores, axis=0, keepdims=True)
        raised = jnp.exp2(scores - peak)
        weights = raised * (1.0 / jnp.sum(raised, axis=0, keepdims=True))
        row_dot = jnp.sum(weights * grad_weights, axis=0, keepdims=True)
        grad_low = (weights * (grad_weights - row_dot) * factor).astype(BF16)
        weights_low = weights.astype(BF16)
        key_terms = dot(grad_low, q, ((1,), (0,)))
        value_terms = dot(weights_low, do, ((1,), (0,)))
        if fresh:
            terms[2 * g] = key_terms
            terms[2 * g + 1] = value_terms
        else:
            terms[2 * g] += key_terms
            terms[2 * g + 1] += value_terms
        back = dot(grad_low, k, ((0,), (0,)))
        for i, c in enumerate(columns):
            grad_query[:, c] = back[i * ROWS : (i + 1) * ROWS]

    def mark(to):
        return jnp.where(wanted == to, 1.0, 0.0).astype(F32)

    before_rows, own_rows, after_rows, global_rows, random_rows = (
        pl.ds(i * ROWS, ROWS) for i in range(5)
    )

    def ret(direction, step, g):
        pair = {4: (far_out, far_in), 3: (far_in, far_in2), 2: (mid_out, mid_in), 1: (near_out, near_in)}
        src, dst = pair[step]
        return remote(
            src.at[direction, g],
            dst.at[direction, g],
            ret_send.at[direction, step - 1, g],
            ret_recv.at[direction, step - 1, g],
            at(direction, 1),
        )

    def global_copy(half, i, source, to):
        return remote(
            global_out.at[half, i],
            global_in.at[half, source],
            global_send.at[half, i],
            global_recv.at[half, source],
            to,
        )

    def edge_copy(g, to):
        part = pl.ds(2 * g, 2)
        return remote(edge_out.at[part], edge_in.at[part], edge_send.at[g], edge_recv.at[g], to)

    def cross_copy(src, dst, send, recv, half, source, to):
        return remote(src.at[half], dst.at[half, source], send.at[half], recv.at[half, source], to)

    def half_rows(i):
        return pl.ds(pl.multiple_of(3 * ROWS + (i % 2) * HALF, HALF), HALF)

    def send_far(g):
        for direction in range(DIRS):
            random = terms[2 * g + PAR[direction], random_rows]
            far_out[direction, g] = (random * mark(at(direction, 4))).astype(BF16)
            ret(direction, 4, g).start()
        for half in range(2):
            for j in range(2):
                i = 2 * g + j
                global_out[half, i] = terms[2 * g + half, pl.ds(3 * ROWS + j * HALF, HALF)].astype(BF16)

                @pl.when(line[half] != i)
                def _():
                    to = i * SIDE + y if half == 0 else z * SIDE + i
                    global_copy(half, i, line[half], to).start()

        @pl.when(y == SIDE - 1)
        def _():
            for half in range(2):
                edge_out[2 * g + half] = terms[2 * g + half, after_rows].astype(BF16)
            edge_copy(g, at(2, 1)).start()

        @pl.when(y == 0)
        def _():
            for half in range(2):
                edge_out[2 * g + half] = terms[2 * g + half, before_rows].astype(BF16)
            edge_copy(g, at(3, 1)).start()

    def pass_far(g):
        for direction in range(DIRS):
            ret(direction, 4, g).wait_recv()
            ret(direction, 3, g).start()

    def send_mid(g):
        for direction in range(DIRS):
            ret(direction, 3, g).wait_recv()
            here = mark(at(direction, 2))
            half = PAR[direction]
            mid_out[direction, g, half] = (
                terms[2 * g + half, random_rows] * here + far_in2[direction, g].astype(F32)
            ).astype(BF16)
            mid_out[direction, g, 1 - half] = (terms[2 * g + 1 - half, random_rows] * here).astype(BF16)
            ret(direction, 2, g).start()

    def send_near(g):
        @pl.when(edge)
        def _():
            edge_copy(g, device).wait_recv()

        for direction in range(DIRS):
            ret(direction, 2, g).wait_recv()
            for half in range(2):
                p = 2 * g + half
                passed = mid_in[direction, g, half].astype(F32)
                if direction == 0:
                    added = jnp.where(
                        y == SIDE - 1,
                        edge_in[p].astype(F32),
                        terms[p, after_rows].astype(BF16).astype(F32),
                    )
                elif direction == 1:
                    added = jnp.where(
                        y == 0,
                        edge_in[p].astype(F32),
                        terms[p, before_rows].astype(BF16).astype(F32),
                    )
                else:
                    added = terms[p, random_rows] * mark(at(direction, 1))
                near_out[direction, g, half] = (passed + added).astype(BF16)
            ret(direction, 1, g).start()

    def add_products(first_head, count):
        total = products[...]
        for i in range(count):
            columns = pl.ds(pl.multiple_of((first_head + i) * HD, HD), HD)
            normed = hidden[:, columns].astype(F32) * inverse
            total = total + grad_query[:, columns] * gain[:, columns] * normed
        products[...] = total

    half_group = per_group // 2

    def group_step(g):
        collect(g)
        assemble(g)
        unit(g, g * per_group, half_group, True)

        @pl.when(g == 0)
        def _():
            forward(4, 1)
            forward(3, 3)
            forward(4, 2)

        add_products(g * per_group, half_group)
        unit(g, g * per_group + half_group, half_group, False)

        @pl.when(g == 0)
        def _():
            forward(4, 3)

        send_far(g)

        @pl.when(g >= 1)
        def _():
            pass_far(g - 1)

        @pl.when(g >= 2)
        def _():
            send_mid(g - 2)

        @pl.when(g >= 3)
        def _():
            send_near(g - 3)

        add_products(g * per_group + half_group, half_group)

    each(0, groups, group_step)

    mean = jnp.sum(products[...], axis=1, keepdims=True) / (heads * HD)

    def hand_copy(part):
        columns = pl.ds(pl.multiple_of(part * (per_group * HD), per_group * HD), per_group * HD)
        return pltpu.make_async_remote_copy(
            src_ref=handed.at[:, columns],
            dst_ref=stream_out.at[0, :, columns],
            send_sem=handed_send.at[part],
            recv_sem=handed_recv.at[part],
            device_id={"section": before},
            device_id_type=MESH,
        )

    def hand(part):
        for i in range(per_group):
            columns = pl.ds(pl.multiple_of((part * per_group + i) * HD, HD), HD)
            normed = hidden[:, columns].astype(F32) * inverse
            grad_norm = grad_query[:, columns] * gain[:, columns]
            grad = inverse * (grad_norm - normed * mean)
            handed[:, columns] = (upstream[:, columns].astype(F32) + grad).astype(BF16)
        hand_copy(part).start()

    each(0, groups, hand)

    for g in range(1, groups):
        if g == 1:
            pass_far(3)
        if g <= 2:
            send_mid(g + 1)
        send_near(g)
        if g == 1:
            for half in range(2):
                start = terms[2 * (line[half] // 2) + half, half_rows(line[half])]

                def add_line(k, total):
                    source = (line[half] + k) % SIDE
                    global_copy(half, 0, source, device).wait_recv()
                    return total + global_in[half, source].astype(F32)

                line_sum[half] = lax.fori_loop(1, SIDE, add_line, start)

                @pl.when(cross[half] != 0)
                def _():
                    line_out[half] = line_sum[half].astype(BF16)
                    to = z * SIDE if half == 0 else y
                    cross_copy(line_out, cross_in, cross_send, cross_recv, half, cross[half], to).start()

        if g == 2:
            for half in range(2):

                @pl.when(cross[half] == 0)
                def _():
                    def add_cross(k, total):
                        cross_copy(line_out, cross_in, cross_send, cross_recv, half, k, device).wait_recv()
                        return total + cross_in[half, k].astype(F32)

                    line_sum[half] = lax.fori_loop(1, SIDE, add_cross, line_sum[half])

                    @pl.when(line[half] != 0)
                    def _():
                        cross_out[half] = line_sum[half].astype(BF16)
                        cross_copy(cross_out, last_in, last_send, last_recv, half, line[half], 0).start()

    @pl.when(device == 0)
    def _():
        for half in range(2):

            def take(i):
                cross_copy(cross_out, last_in, last_send, last_recv, half, i, device).wait_recv()
                rows = pl.ds(pl.multiple_of(ROWS + (i % 2) * HALF, HALF), HALF)
                terms[2 * (i // 2) + half, rows] += last_in[half, i].astype(F32)

            each(1, SIDE, take)
            terms[half, pl.ds(ROWS, HALF)] += line_sum[half]

    for g in range(groups):
        for direction in range(DIRS):
            ret(direction, 1, g).wait_recv()
        for half, out in ((0, key_out), (1, value_out)):
            total = terms[2 * g + half, own_rows]
            for direction in range(DIRS):
                total = total + near_in[direction, g, half].astype(F32)
            out[0, :, pl.ds(g * HD, HD)] = total.astype(BF16)

    def sent(g):
        for direction in range(DIRS):
            for step in (1, 2, 3, 4):
                kv(direction, step, g).wait_send()
                ret(direction, step, g).wait_send()

        @pl.when(edge)
        def _():
            halo_copy(g, 0, device).wait_send()
            edge_copy(g, device).wait_send()

    each(0, groups, sent)

    for half in range(2):

        def sent_pieces(k):
            corner_copy(2, half, 0, device, k).wait_send()
            global_copy(half, (line[half] + k) % SIDE, 0, device).wait_send()

        each(1, SIDE, sent_pieces)

        @pl.when(cross[half] == 0)
        def _():
            def sent_across(k):
                corner_copy(1, half, 0, device, k).wait_send()

            each(1, SIDE, sent_across)

            @pl.when(line[half] != 0)
            def _():
                cross_copy(cross_out, last_in, last_send, last_recv, half, 0, device).wait_send()

        @pl.when(cross[half] != 0)
        def _():
            cross_copy(line_out, cross_in, cross_send, cross_recv, half, 0, device).wait_send()

    @pl.when(device == 0)
    def _():
        def sent_corner(i):
            for half in range(2):
                corner_copy(0, half, i, device, i).wait_send()

        each(1, SIDE, sent_corner)

    for part in range(groups):
        hand_copy(part).wait()


def solution(mesh):
    def on_device(stream, cotangent, keys, values, gain, rand_blocks):
        heads = stream.shape[2] // HD
        groups = keys.shape[2] // HD
        pieces = 2 * groups
        block = (ROWS, HD)
        part = (HALF, HD)
        vmem = pl.BlockSpec(memory_space=pltpu.VMEM)
        hbm = pl.BlockSpec(memory_space=pl.ANY)
        dma = pltpu.SemaphoreType.DMA

        def bf16(*shape):
            return pltpu.VMEM(shape, BF16)

        def f32(*shape):
            return pltpu.VMEM(shape, F32)

        def body(*refs):
            kernel(heads, groups, *refs)

        return pl.pallas_call(
            body,
            name="relay",
            out_shape=(
                jax.ShapeDtypeStruct(stream.shape, BF16),
                jax.ShapeDtypeStruct(keys.shape, BF16),
                jax.ShapeDtypeStruct(values.shape, BF16),
            ),
            in_specs=[pl.BlockSpec(memory_space=pltpu.SMEM), hbm, hbm, hbm, hbm, hbm],
            out_specs=(hbm, vmem, vmem),
            scratch_shapes=[
                f32(1, heads * HD),
                bf16(ROWS, heads * HD),
                bf16(ROWS, heads * HD),
                bf16(ROWS, heads * HD),
                f32(ROWS, heads * HD),
                bf16(ROWS, heads * HD),
                f32(*block),
                bf16(2 * SIDE, pieces, *block),
                bf16(2, SIDE, *part),
                bf16(pieces, *block),
                bf16(groups, 5 * ROWS, HD),
                bf16(groups, 5 * ROWS, HD),
                f32(pieces, 5 * ROWS, HD),
                bf16(DIRS, groups, *block),
                bf16(DIRS, groups, *block),
                bf16(DIRS, groups, *block),
                bf16(DIRS, groups, 2, *block),
                bf16(DIRS, groups, 2, *block),
                bf16(DIRS, groups, 2, *block),
                bf16(DIRS, groups, 2, *block),
                bf16(pieces, *block),
                bf16(pieces, *block),
                bf16(2, SIDE, *part),
                bf16(2, SIDE, *part),
                f32(2, *part),
                bf16(2, *part),
                bf16(2, SIDE, *part),
                bf16(2, *part),
                bf16(2, SIDE, *part),
                dma((pieces + 3,)),
                dma((DIRS, 4, groups)),
                dma((DIRS, 4, groups)),
                dma((groups,)),
                dma((groups,)),
                dma((3, 2, SIDE)),
                dma((2, SIDE)),
                dma((DIRS, 4, groups)),
                dma((DIRS, 4, groups)),
                dma((groups,)),
                dma((groups,)),
                dma((2, SIDE)),
                dma((2, SIDE)),
                dma((2,)),
                dma((2, SIDE)),
                dma((2,)),
                dma((2, SIDE)),
                dma((groups,)),
                dma((groups,)),
            ],
            compiler_params=pltpu.CompilerParams(
                collective_id=0, has_side_effects=True, vmem_limit_bytes=60 * 1024 * 1024
            ),
        )(rand_blocks, gain, stream, cotangent, keys, values)

    return jax.shard_map(
        on_device,
        mesh=mesh,
        in_specs=(
            P("section", "seq", None),
            P("section", "seq", None),
            P("section", "seq", None),
            P("section", "seq", None),
            P("section", None),
            P("seq", None),
        ),
        out_specs=(P("section", "seq", None), P("section", "seq", None), P("section", "seq", None)),
        check_vma=False,
    )
```

time: 100 us -> 83.8 us (0.84)
  Pallas kernels: 91.5 us -> 78.4 us
  local copies, waits for them, and re-layouts: 7.25 us -> 3.93 us
    pallas_call x1, Pallas kernels: 91.5 us -> 78.4 us  [on_device(): pl.pallas_call(body, name='relay', out_shape=(jax.ShapeDtypeStruct(stream...]
    unnamed x13 -> x7, local copies, waits for them, and re-layouts: 7.25 us -> 3.93 us
where the time goes in v2:
time: 83.8 us; the launch traced here: 83.6 us
  Pallas kernels  78.4 us (94%)
  local copies, waits for them, and re-layouts  3.93 us (5%)
  between operations  1.3 us (2%)
    pallas_call x1, Pallas kernels, on_device(): pl.pallas_call(body, name='relay', out_shape=(jax.ShapeDtypeStruct(stream...  78.4 us
    unnamed x7, local copies, waits for them, and re-layouts  3.93 us

profile of v2, /device:TPU:6, one launch (start us, length us, event | category | flops | bytes accessed | tf_op | source)
XLA Modules:
  0.0 83.6 jit_solution(16883740787183616737)
XLA Ops:
  1.3 78.4 %relay.1 = (bf16[1,128,4096]{2,1,0:T(8,128)(2,1)}, bf16[1,128,512]{2,1,0:T(8,128)(2,1)}, bf16[1,128,512]{2,1,0:T(8,128)(2,1)}) custom-call(s32[1,1]{1,0:T(1,128)S(6)} %copy.12.refs_0_, f32[1,4096]{1,0:T(1,128)} %refs_1_.1, bf16[1,128,4096]{2,1,0:T(8,128)(2,1)} %refs_2_.1, bf16[1,128,4096]{2,1,0:T(8,128)(2,1)} %refs_3_.1, bf16[1,128,512]{2,1,0:T(8,128)(2,1)} %refs_4_.1, ...), custom_call_target="tpu_custom_call" | custom-call | tf_op jit(solution)/shard_map/relay/pallas_call | solution.py:654
  79.7 0.0 copy-start.1
  79.7 2.3 %copy.13 = bf16[1,128,4096]{2,1,0:T(8,128)(2,1)} copy(bf16[1,128,4096]{2,1,0:T(8,128)(2,1)} %get-tuple-element.6) | data formatting | bytes 2097152
  82.0 0.0 copy-done.1
  82.0 0.0 copy-start
  82.0 0.7 copy.14
  82.7 0.3 copy-done
  83.0 0.7 copy.15
Async XLA Ops:
  79.7 2.3 %copy-start.1 = (bf16[1,128,512]{2,1,0:T(8,128)(2,1)S(1)}, bf16[1,128,512]{2,1,0:T(8,128)(2,1)}, u32[]{:S(2)}) copy-start(bf16[1,128,512]{2,1,0:T(8,128)(2,1)} %get-tuple-element.7) | copy-start | bytes 393220
  82.0 1.0 %copy-start = (bf16[1,128,512]{2,1,0:T(8,128)(2,1)S(1)}, bf16[1,128,512]{2,1,0:T(8,128)(2,1)}, u32[]{:S(2)}) copy-start(bf16[1,128,512]{2,1,0:T(8,128)(2,1)} %get-tuple-element.8) | copy-start | bytes 393220

commit v3 on v2

--- a/solution.py
+++ b/solution.py
@@ -11,9 +11,11 @@
 HD = 128
 ROWS = 128
 HALF = ROWS // 2
+SQUARE = 4
 NEG = -1e30
 F32 = jnp.float32
 BF16 = jnp.bfloat16
+VMEM_LIMIT = 48 * 1024 * 1024
 SIDE = 8
 DIRS = 4
 PAR = (0, 1, 0, 1)
@@ -41,6 +43,10 @@
     queries,
     grad_query,
     handed,
+    arrived,
+    hidden_after,
+    mean_out,
+    mean_in,
     products,
     blocks,
     corner,
@@ -83,6 +89,8 @@
     last_recv,
     handed_send,
     handed_recv,
+    hidden_sem,
+    mean_sem,
 ):
     device = lax.axis_index("seq")
     section = lax.axis_index("section")
@@ -179,8 +187,39 @@
     def slot(direction, step):
         return (step, SIDE - step, SIDE + step, 2 * SIDE - step)[direction]
 
-    def kv(direction, step, g):
-        part = pl.ds(2 * g, 2) if step <= 2 else pl.ds(2 * g + PAR[direction], 1)
+    def both_halves(condition, direction, step, g, act):
+        if condition is None:
+            act(direction, step, g, step <= 2)
+            return
+
+        @pl.when(condition)
+        def _():
+            act(direction, step, g, True)
+
+        @pl.when(jnp.logical_not(condition))
+        def _():
+            act(direction, step, g, False)
+
+    def middle(i):
+        return (i % SQUARE == 1) | (i % SQUARE == 2)
+
+    def kv_whole(direction, step, sender):
+        if step > 2:
+            return None
+        if step == 2:
+            if sender:
+                return middle(y if direction < 2 else z)
+            return middle((y + SIDE - 1, y + 1, z + SIDE - 1, z + 1)[direction])
+        if direction == 0:
+            return y != (SIDE - 1 if sender else 0)
+        if direction == 1:
+            return y != (0 if sender else SIDE - 1)
+        if direction == 2:
+            return (z % SQUARE != (3 if sender else 0)) | (y == SIDE - 1)
+        return (z % SQUARE != (0 if sender else 3)) | (y == 0)
+
+    def kv(direction, step, g, whole):
+        part = pl.ds(2 * g, 2) if whole else pl.ds(2 * g + PAR[direction], 1)
         src = blocks.at[0 if step == 1 else slot(direction, step - 1), part]
         return remote(
             src,
@@ -190,6 +229,15 @@
             at(direction, 1),
         )
 
+    def kv_start(*what):
+        kv(*what).start()
+
+    def kv_arrived(*what):
+        kv(*what).wait_recv()
+
+    def kv_left(*what):
+        kv(*what).wait_send()
+
     def halo_copy(g, source, to):
         part = pl.ds(2 * g, 2)
         return remote(blocks.at[source, part], halo.at[part], halo_send.at[g], halo_recv.at[g], to)
@@ -197,8 +245,8 @@
     def forward(step, g):
         for direction in range(DIRS):
             if step > 1:
-                kv(direction, step - 1, g).wait_recv()
-            kv(direction, step, g).start()
+                both_halves(kv_whole(direction, step - 1, False), direction, step - 1, g, kv_arrived)
+            both_halves(kv_whole(direction, step, True), direction, step, g, kv_start)
         if step == 2:
 
             @pl.when(y == SIDE - 1)
@@ -211,6 +259,17 @@
 
     forward(1, 0)
     forward(1, 1)
+    forward(1, 2)
+
+    hidden_copy = pltpu.make_async_remote_copy(
+        src_ref=stream.at[0],
+        dst_ref=hidden_after,
+        send_sem=hidden_sem.at[0],
+        recv_sem=hidden_sem.at[1],
+        device_id={"section": before},
+        device_id_type=MESH,
+    )
+    hidden_copy.start()
 
     load_hidden.wait()
 
@@ -231,8 +290,8 @@
     products[...] = jnp.zeros_like(products)
 
     forward(2, 0)
-    forward(1, 2)
     forward(2, 1)
+    forward(1, 3)
 
     for half in range(2):
 
@@ -248,10 +307,9 @@
             each(1, SIDE, spread)
 
     forward(3, 0)
-    forward(1, 3)
     forward(2, 2)
+    forward(3, 1)
     forward(4, 0)
-    forward(3, 1)
 
     for half in range(2):
 
@@ -270,7 +328,7 @@
 
     def collect(g):
         for direction in range(DIRS):
-            kv(direction, 4, g).wait_recv()
+            kv(direction, 4, g, False).wait_recv()
 
         @pl.when(edge)
         def _():
@@ -353,16 +411,59 @@
         pl.ds(i * ROWS, ROWS) for i in range(5)
     )
 
-    def ret(direction, step, g):
+    def ret_whole(direction, step, sender):
+        if step > 2:
+            return None
+        if step == 2:
+            i = y if direction < 2 else z
+            if not sender:
+                i = i + (SIDE - 1, 1, SIDE - 1, 1)[direction]
+            low = (i % SQUARE) < 2
+            return low if direction in (0, 2) else jnp.logical_not(low)
+        if direction == 0:
+            return y != (SIDE - 1 if sender else 0)
+        if direction == 1:
+            return y != (0 if sender else SIDE - 1)
+        if direction == 2:
+            return (z % SQUARE != (3 if sender else 0)) | (y == 0)
+        return (z % SQUARE != (0 if sender else 3)) | (y == SIDE - 1)
+
+    def ret(direction, step, g, whole):
         pair = {4: (far_out, far_in), 3: (far_in, far_in2), 2: (mid_out, mid_in), 1: (near_out, near_in)}
         src, dst = pair[step]
+        if step > 2:
+            src, dst = src.at[direction, g], dst.at[direction, g]
+        else:
+            part = pl.ds(0, 2) if whole else pl.ds(PAR[direction], 1)
+            src, dst = src.at[direction, g, part], dst.at[direction, g, part]
         return remote(
-            src.at[direction, g],
-            dst.at[direction, g],
+            src,
+            dst,
             ret_send.at[direction, step - 1, g],
             ret_recv.at[direction, step - 1, g],
             at(direction, 1),
         )
+
+    def ret_start(direction, step, g):
+        def start(*what):
+            ret(*what).start()
+
+        both_halves(ret_whole(direction, step, True), direction, step, g, start)
+
+    def ret_arrived(direction, step, g):
+        def wait(*what):
+            ret(*what).wait_recv()
+
+        both_halves(ret_whole(direction, step, False), direction, step, g, wait)
+
+    def ret_left(*what):
+        ret(*what).wait_send()
+
+    def received(buffer, direction, step, g, half):
+        value = buffer[direction, g, half].astype(F32)
+        if half == PAR[direction]:
+            return value
+        return jnp.where(ret_whole(direction, step, False), value, 0.0)
 
     def global_copy(half, i, source, to):
         return remote(
@@ -387,7 +488,7 @@
         for direction in range(DIRS):
             random = terms[2 * g + PAR[direction], random_rows]
             far_out[direction, g] = (random * mark(at(direction, 4))).astype(BF16)
-            ret(direction, 4, g).start()
+            ret_start(direction, 4, g)
         for half in range(2):
             for j in range(2):
                 i = 2 * g + j
@@ -402,29 +503,29 @@
         def _():
             for half in range(2):
                 edge_out[2 * g + half] = terms[2 * g + half, after_rows].astype(BF16)
-            edge_copy(g, at(2, 1)).start()
+            edge_copy(g, z * SIDE).start()
 
         @pl.when(y == 0)
         def _():
             for half in range(2):
                 edge_out[2 * g + half] = terms[2 * g + half, before_rows].astype(BF16)
-            edge_copy(g, at(3, 1)).start()
+            edge_copy(g, z * SIDE + SIDE - 1).start()
 
     def pass_far(g):
         for direction in range(DIRS):
-            ret(direction, 4, g).wait_recv()
-            ret(direction, 3, g).start()
+            ret_arrived(direction, 4, g)
+            ret_start(direction, 3, g)
 
     def send_mid(g):
         for direction in range(DIRS):
-            ret(direction, 3, g).wait_recv()
+            ret_arrived(direction, 3, g)
             here = mark(at(direction, 2))
             half = PAR[direction]
             mid_out[direction, g, half] = (
                 terms[2 * g + half, random_rows] * here + far_in2[direction, g].astype(F32)
             ).astype(BF16)
             mid_out[direction, g, 1 - half] = (terms[2 * g + 1 - half, random_rows] * here).astype(BF16)
-            ret(direction, 2, g).start()
+            ret_start(direction, 2, g)
 
     def send_near(g):
         @pl.when(edge)
@@ -432,33 +533,50 @@
             edge_copy(g, device).wait_recv()
 
         for direction in range(DIRS):
-            ret(direction, 2, g).wait_recv()
+            ret_arrived(direction, 2, g)
             for half in range(2):
                 p = 2 * g + half
-                passed = mid_in[direction, g, half].astype(F32)
-                if direction == 0:
+                passed = received(mid_in, direction, 2, g, half)
+                if direction < 2:
+                    rows = after_rows if direction == 0 else before_rows
                     added = jnp.where(
-                        y == SIDE - 1,
-                        edge_in[p].astype(F32),
-                        terms[p, after_rows].astype(BF16).astype(F32),
-                    )
-                elif direction == 1:
-                    added = jnp.where(
-                        y == 0,
-                        edge_in[p].astype(F32),
-                        terms[p, before_rows].astype(BF16).astype(F32),
+                        y == (SIDE - 1 if direction == 0 else 0),
+                        0.0,
+                        terms[p, rows].astype(BF16).astype(F32),
                     )
                 else:
-                    added = terms[p, random_rows] * mark(at(direction, 1))
+                    added = terms[p, random_rows] * mark(at(direction, 1)) + jnp.where(
+                        y == (0 if direction == 2 else SIDE - 1), edge_in[p].astype(F32), 0.0
+                    )
                 near_out[direction, g, half] = (passed + added).astype(BF16)
-            ret(direction, 1, g).start()
-
-    def add_products(first_head, count):
+            ret_start(direction, 1, g)
+
+    def to_before(src, dst, send, recv):
+        return pltpu.make_async_remote_copy(
+            src_ref=src,
+            dst_ref=dst,
+            send_sem=send,
+            recv_sem=recv,
+            device_id={"section": before},
+            device_id_type=MESH,
+        )
+
+    def hand_copy(part):
+        columns = pl.ds(pl.multiple_of(part * (per_group * HD), per_group * HD), per_group * HD)
+        return to_before(
+            handed.at[:, columns], arrived.at[:, columns], handed_send.at[part], handed_recv.at[part]
+        )
+
+    def mean_copy():
+        return to_before(mean_out, mean_in, mean_sem.at[0], mean_sem.at[1])
+
+    def hand(first_head, count):
         total = products[...]
         for i in range(count):
             columns = pl.ds(pl.multiple_of((first_head + i) * HD, HD), HD)
-            normed = hidden[:, columns].astype(F32) * inverse
-            total = total + grad_query[:, columns] * gain[:, columns] * normed
+            grad_norm = grad_query[:, columns] * gain[:, columns]
+            total = total + grad_norm * (hidden[:, columns].astype(F32) * inverse)
+            handed[:, columns] = (upstream[:, columns].astype(F32) + inverse * grad_norm).astype(BF16)
         products[...] = total
 
     half_group = per_group // 2
@@ -468,20 +586,24 @@
         assemble(g)
         unit(g, g * per_group, half_group, True)
 
+
         @pl.when(g == 0)
         def _():
             forward(4, 1)
             forward(3, 3)
             forward(4, 2)
 
-        add_products(g * per_group, half_group)
+        hand(g * per_group, half_group)
         unit(g, g * per_group + half_group, half_group, False)
 
+        send_far(g)
+
         @pl.when(g == 0)
         def _():
             forward(4, 3)
 
-        send_far(g)
+        hand(g * per_group + half_group, half_group)
+        hand_copy(g).start()
 
         @pl.when(g >= 1)
         def _():
@@ -495,39 +617,32 @@
         def _():
             send_near(g - 3)
 
-        add_products(g * per_group + half_group, half_group)
-
     each(0, groups, group_step)
 
     mean = jnp.sum(products[...], axis=1, keepdims=True) / (heads * HD)
-
-    def hand_copy(part):
-        columns = pl.ds(pl.multiple_of(part * (per_group * HD), per_group * HD), per_group * HD)
-        return pltpu.make_async_remote_copy(
-            src_ref=handed.at[:, columns],
-            dst_ref=stream_out.at[0, :, columns],
-            send_sem=handed_send.at[part],
-            recv_sem=handed_recv.at[part],
-            device_id={"section": before},
-            device_id_type=MESH,
-        )
-
-    def hand(part):
-        for i in range(per_group):
-            columns = pl.ds(pl.multiple_of((part * per_group + i) * HD, HD), HD)
-            normed = hidden[:, columns].astype(F32) * inverse
-            grad_norm = grad_query[:, columns] * gain[:, columns]
-            grad = inverse * (grad_norm - normed * mean)
-            handed[:, columns] = (upstream[:, columns].astype(F32) + grad).astype(BF16)
-        hand_copy(part).start()
-
-    each(0, groups, hand)
+    mean_out[...] = jnp.broadcast_to(inverse * inverse * mean, (ROWS, HD))
+    mean_copy().start()
+
+    def receive_hand():
+        hidden_copy.wait_recv()
+        mean_copy().wait_recv()
+        for part in range(groups):
+            hand_copy(part).wait_recv()
+
+        def finish(h):
+            columns = pl.ds(pl.multiple_of(h * HD, HD), HD)
+            along_input = hidden_after[:, columns].astype(F32) * mean_in[...]
+            stream_out[0, :, columns] = (arrived[:, columns].astype(F32) - along_input).astype(BF16)
+
+        each(0, heads, finish)
 
     for g in range(1, groups):
         if g == 1:
             pass_far(3)
         if g <= 2:
             send_mid(g + 1)
+        if g == 3:
+            receive_hand()
         send_near(g)
         if g == 1:
             for half in range(2):
@@ -576,18 +691,18 @@
 
     for g in range(groups):
         for direction in range(DIRS):
-            ret(direction, 1, g).wait_recv()
+            ret_arrived(direction, 1, g)
         for half, out in ((0, key_out), (1, value_out)):
             total = terms[2 * g + half, own_rows]
             for direction in range(DIRS):
-                total = total + near_in[direction, g, half].astype(F32)
+                total = total + received(near_in, direction, 1, g, half)
             out[0, :, pl.ds(g * HD, HD)] = total.astype(BF16)
 
     def sent(g):
         for direction in range(DIRS):
             for step in (1, 2, 3, 4):
-                kv(direction, step, g).wait_send()
-                ret(direction, step, g).wait_send()
+                both_halves(kv_whole(direction, step, True), direction, step, g, kv_left)
+                both_halves(ret_whole(direction, step, True), direction, step, g, ret_left)
 
         @pl.when(edge)
         def _():
@@ -627,8 +742,10 @@
 
         each(1, SIDE, sent_corner)
 
+    hidden_copy.wait_send()
+    mean_copy().wait_send()
     for part in range(groups):
-        hand_copy(part).wait()
+        hand_copy(part).wait_send()
 
 
 def solution(mesh):
@@ -639,7 +756,7 @@
         block = (ROWS, HD)
         part = (HALF, HD)
         vmem = pl.BlockSpec(memory_space=pltpu.VMEM)
-        hbm = pl.BlockSpec(memory_space=pl.ANY)
+        hbm = pl.BlockSpec(memory_space=pltpu.HBM)
         dma = pltpu.SemaphoreType.DMA
 
         def bf16(*shape):
@@ -648,10 +765,13 @@
         def f32(*shape):
             return pltpu.VMEM(shape, F32)
 
+        def in_hbm(array):
+            return pltpu.with_memory_space_constraint(array, pltpu.HBM)
+
         def body(*refs):
             kernel(heads, groups, *refs)
 
-        return pl.pallas_call(
+        results = pl.pallas_call(
             body,
             name="relay",
             out_shape=(
@@ -660,7 +780,7 @@
                 jax.ShapeDtypeStruct(values.shape, BF16),
             ),
             in_specs=[pl.BlockSpec(memory_space=pltpu.SMEM), hbm, hbm, hbm, hbm, hbm],
-            out_specs=(hbm, vmem, vmem),
+            out_specs=(vmem, vmem, vmem),
             scratch_shapes=[
                 f32(1, heads * HD),
                 bf16(ROWS, heads * HD),
@@ -668,6 +788,10 @@
                 bf16(ROWS, heads * HD),
                 f32(ROWS, heads * HD),
                 bf16(ROWS, heads * HD),
+                bf16(ROWS, heads * HD),
+                bf16(ROWS, heads * HD),
+                f32(*block),
+                f32(*block),
                 f32(*block),
                 bf16(2 * SIDE, pieces, *block),
                 bf16(2, SIDE, *part),
@@ -710,11 +834,34 @@
                 dma((2, SIDE)),
                 dma((groups,)),
                 dma((groups,)),
+                dma((2,)),
+                dma((2,)),
             ],
             compiler_params=pltpu.CompilerParams(
-                collective_id=0, has_side_effects=True, vmem_limit_bytes=60 * 1024 * 1024
+                collective_id=0, has_side_effects=True, vmem_limit_bytes=VMEM_LIMIT
             ),
-        )(rand_blocks, gain, stream, cotangent, keys, values)
+        )(rand_blocks, *(in_hbm(a) for a in (gain, stream, cotangent, keys, values)))
+
+        def write(*refs):
+            sources, targets, sems = refs[:3], refs[3:6], refs[6]
+            copies = [
+                pltpu.make_async_copy(src, dst, sems.at[i])
+                for i, (src, dst) in enumerate(zip(sources, targets))
+            ]
+            for copy in copies:
+                copy.start()
+            for copy in copies:
+                copy.wait()
+
+        return pl.pallas_call(
+            write,
+            name="write",
+            out_shape=tuple(jax.ShapeDtypeStruct(r.shape, r.dtype) for r in results),
+            in_specs=[pl.BlockSpec(memory_space=pl.ANY)] * 3,
+            out_specs=(hbm,) * 3,
+            scratch_shapes=[dma((3,))],
+            compiler_params=pltpu.CompilerParams(vmem_limit_bytes=1024 * 1024),
+        )(*results)
 
     return jax.shard_map(
         on_device,

time: 83.8 us -> 75.7 us (0.903)
  Pallas kernels: 78.4 us -> 73.7 us
  local copies, waits for them, and re-layouts: 3.93 us -> 0 us
    pallas_call x1, Pallas kernels: 78.4 us -> 72.6 us  [on_device(): pl.pallas_call(body, name='relay', out_shape=(jax.ShapeDtypeStruct(stream...]
    unnamed x7 -> x0, local copies, waits for them, and re-layouts: 3.93 us -> none
    pallas_call x0 -> x1, Pallas kernels: none -> 1.07 us  [on_device(): pl.pallas_call(write, name='write', out_shape=tuple((jax.ShapeDtypeStruct...]
where the time goes in v3:
time: 75.7 us; the launch traced here: 75 us
  Pallas kernels  73.7 us (97%)
  between operations  1.29 us (2%)
    pallas_call x1, Pallas kernels, on_device(): pl.pallas_call(body, name='relay', out_shape=(jax.ShapeDtypeStruct(stream...  72.6 us

profile of v3, /device:TPU:6, one launch (start us, length us, event | category | flops | bytes accessed | tf_op | source)
XLA Modules:
  0.0 75.0 jit_solution(5982288990371668202)
XLA Ops:
  1.3 72.6 %relay.1 = (bf16[1,128,4096]{2,1,0:T(8,128)(2,1)S(1)}, bf16[1,128,512]{2,1,0:T(8,128)(2,1)S(1)}, bf16[1,128,512]{2,1,0:T(8,128)(2,1)S(1)}) custom-call(s32[1,1]{1,0:T(1,128)S(6)} %copy.9.refs_0_, f32[1,4096]{1,0:T(1,128)} %refs_1_.1, bf16[1,128,4096]{2,1,0:T(8,128)(2,1)} %refs_2_.1, bf16[1,128,4096]{2,1,0:T(8,128)(2,1)} %refs_3_.1, ...), custom_call_target="tpu_custom_call" | custom-call | tf_op jit(solution)/shard_map/relay/pallas_call | solution.py:774
  73.9 1.1 %write.1 = (bf16[1,128,4096]{2,1,0:T(8,128)(2,1)}, bf16[1,128,512]{2,1,0:T(8,128)(2,1)}, bf16[1,128,512]{2,1,0:T(8,128)(2,1)}) custom-call(bf16[1,128,4096]{2,1,0:T(8,128)(2,1)S(1)} %get-tuple-element.6.refs_0_, bf16[1,128,512]{2,1,0:T(8,128)(2,1)S(1)} %get-tuple-element.7.refs_1_, bf16[1,128,512]{2,1,0:T(8,128)(2,1)S(1)} %get-tuple-element.8.refs_2_), custom_call_target="tpu_custom_call" | custom-call | tf_op jit(solution)/shard_map/write/pallas_call | solution.py:856

commit v4 on v3

--- a/solution.py
+++ b/solution.py
@@ -257,9 +257,7 @@
             def _():
                 halo_copy(g, 2 * SIDE - 1, z * SIDE + SIDE - 1).start()
 
-    forward(1, 0)
-    forward(1, 1)
-    forward(1, 2)
+    each(0, groups, lambda g: forward(1, g))
 
     hidden_copy = pltpu.make_async_remote_copy(
         src_ref=stream.at[0],
@@ -291,7 +289,6 @@
 
     forward(2, 0)
     forward(2, 1)
-    forward(1, 3)
 
     for half in range(2):
 
@@ -306,10 +303,9 @@
 
             each(1, SIDE, spread)
 
+    forward(2, 2)
     forward(3, 0)
-    forward(2, 2)
-    forward(3, 1)
-    forward(4, 0)
+    forward(2, 3)
 
     for half in range(2):
 
@@ -322,8 +318,12 @@
             corner_copy(2, half, line[half], at(along[half], k), k).start()
 
     each(1, SIDE, over_lines)
-    forward(2, 3)
+    forward(3, 1)
     forward(3, 2)
+    forward(4, 0)
+    forward(3, 3)
+    forward(4, 1)
+    forward(4, 2)
     load_upstream.wait()
 
     def collect(g):
@@ -388,10 +388,10 @@
         scores = jnp.concatenate(scores, axis=0)
         peak = jnp.max(scores, axis=0, keepdims=True)
         raised = jnp.exp2(scores - peak)
-        weights = raised * (1.0 / jnp.sum(raised, axis=0, keepdims=True))
-        row_dot = jnp.sum(weights * grad_weights, axis=0, keepdims=True)
-        grad_low = (weights * (grad_weights - row_dot) * factor).astype(BF16)
-        weights_low = weights.astype(BF16)
+        share = 1.0 / jnp.sum(raised, axis=0, keepdims=True)
+        row_dot = jnp.sum(raised * grad_weights, axis=0, keepdims=True) * share
+        grad_low = ((raised * (share * factor)) * (grad_weights - row_dot)).astype(BF16)
+        weights_low = (raised * share).astype(BF16)
         key_terms = dot(grad_low, q, ((1,), (0,)))
         value_terms = dot(weights_low, do, ((1,), (0,)))
         if fresh:
@@ -485,19 +485,20 @@
         return pl.ds(pl.multiple_of(3 * ROWS + (i % 2) * HALF, HALF), HALF)
 
     def send_far(g):
+        for half in range(2):
+            for j in range(2):
+                i = 2 * g + j
+                global_out[half, i] = terms[2 * g + half, pl.ds(3 * ROWS + j * HALF, HALF)].astype(BF16)
+
+                @pl.when(line[half] != i)
+                def _():
+                    to = i * SIDE + y if half == 0 else z * SIDE + i
+                    global_copy(half, i, line[half], to).start()
+
         for direction in range(DIRS):
             random = terms[2 * g + PAR[direction], random_rows]
             far_out[direction, g] = (random * mark(at(direction, 4))).astype(BF16)
             ret_start(direction, 4, g)
-        for half in range(2):
-            for j in range(2):
-                i = 2 * g + j
-                global_out[half, i] = terms[2 * g + half, pl.ds(3 * ROWS + j * HALF, HALF)].astype(BF16)
-
-                @pl.when(line[half] != i)
-                def _():
-                    to = i * SIDE + y if half == 0 else z * SIDE + i
-                    global_copy(half, i, line[half], to).start()
 
         @pl.when(y == SIDE - 1)
         def _():
@@ -589,19 +590,12 @@
 
         @pl.when(g == 0)
         def _():
-            forward(4, 1)
-            forward(3, 3)
-            forward(4, 2)
+            forward(4, 3)
 
         hand(g * per_group, half_group)
         unit(g, g * per_group + half_group, half_group, False)
 
         send_far(g)
-
-        @pl.when(g == 0)
-        def _():
-            forward(4, 3)
-
         hand(g * per_group + half_group, half_group)
         hand_copy(g).start()
 
@@ -622,6 +616,22 @@
     mean = jnp.sum(products[...], axis=1, keepdims=True) / (heads * HD)
     mean_out[...] = jnp.broadcast_to(inverse * inverse * mean, (ROWS, HD))
     mean_copy().start()
+
+    def add_crosses():
+        for half in range(2):
+
+            @pl.when(cross[half] == 0)
+            def _():
+                def add_cross(k, total):
+                    cross_copy(line_out, cross_in, cross_send, cross_recv, half, k, device).wait_recv()
+                    return total + cross_in[half, k].astype(F32)
+
+                line_sum[half] = lax.fori_loop(1, SIDE, add_cross, line_sum[half])
+
+                @pl.when(line[half] != 0)
+                def _():
+                    cross_out[half] = line_sum[half].astype(BF16)
+                    cross_copy(cross_out, last_in, last_send, last_recv, half, line[half], 0).start()
 
     def receive_hand():
         hidden_copy.wait_recv()
@@ -643,6 +653,7 @@
             send_mid(g + 1)
         if g == 3:
             receive_hand()
+            add_crosses()
         send_near(g)
         if g == 1:
             for half in range(2):
@@ -660,22 +671,6 @@
                     line_out[half] = line_sum[half].astype(BF16)
                     to = z * SIDE if half == 0 else y
                     cross_copy(line_out, cross_in, cross_send, cross_recv, half, cross[half], to).start()
-
-        if g == 2:
-            for half in range(2):
-
-                @pl.when(cross[half] == 0)
-                def _():
-                    def add_cross(k, total):
-                        cross_copy(line_out, cross_in, cross_send, cross_recv, half, k, device).wait_recv()
-                        return total + cross_in[half, k].astype(F32)
-
-                    line_sum[half] = lax.fori_loop(1, SIDE, add_cross, line_sum[half])
-
-                    @pl.when(line[half] != 0)
-                    def _():
-                        cross_out[half] = line_sum[half].astype(BF16)
-                        cross_copy(cross_out, last_in, last_send, last_recv, half, line[half], 0).start()
 
     @pl.when(device == 0)
     def _():

time: 75.7 us -> 74.2 us (0.980)
  Pallas kernels: 73.7 us -> 72.8 us
    pallas_call x1, Pallas kernels: 72.6 us -> 71.7 us  [on_device(): pl.pallas_call(body, name='relay', out_shape=(jax.ShapeDtypeStruct(stream...]
where the time goes in v4:
time: 74.2 us; the launch traced here: 74.1 us
  Pallas kernels  72.8 us (98%)
  between operations  1.29 us (2%)
    pallas_call x1, Pallas kernels, on_device(): pl.pallas_call(body, name='relay', out_shape=(jax.ShapeDtypeStruct(stream...  71.7 us

profile of v4, /device:TPU:6, one launch (start us, length us, event | category | flops | bytes accessed | tf_op | source)
XLA Modules:
  0.0 74.1 jit_solution(14286381962016643582)
XLA Ops:
  1.3 71.7 %relay.1 = (bf16[1,128,4096]{2,1,0:T(8,128)(2,1)S(1)}, bf16[1,128,512]{2,1,0:T(8,128)(2,1)S(1)}, bf16[1,128,512]{2,1,0:T(8,128)(2,1)S(1)}) custom-call(s32[1,1]{1,0:T(1,128)S(6)} %copy.9.refs_0_, f32[1,4096]{1,0:T(1,128)} %refs_1_.1, bf16[1,128,4096]{2,1,0:T(8,128)(2,1)} %refs_2_.1, bf16[1,128,4096]{2,1,0:T(8,128)(2,1)} %refs_3_.1, ...), custom_call_target="tpu_custom_call" | custom-call | tf_op jit(solution)/shard_map/relay/pallas_call | solution.py:769
  73.0 1.1 %write.1 = (bf16[1,128,4096]{2,1,0:T(8,128)(2,1)}, bf16[1,128,512]{2,1,0:T(8,128)(2,1)}, bf16[1,128,512]{2,1,0:T(8,128)(2,1)}) custom-call(bf16[1,128,4096]{2,1,0:T(8,128)(2,1)S(1)} %get-tuple-element.6.refs_0_, bf16[1,128,512]{2,1,0:T(8,128)(2,1)S(1)} %get-tuple-element.7.refs_1_, bf16[1,128,512]{2,1,0:T(8,128)(2,1)S(1)} %get-tuple-element.8.refs_2_), custom_call_target="tpu_custom_call" | custom-call | tf_op jit(solution)/shard_map/write/pallas_call | solution.py:851

commit v5 on v4

--- a/solution.py
+++ b/solution.py
@@ -374,7 +374,7 @@
     bias = (no_before, None, no_after, no_before, None)
     scale = factor * math.log2(math.e)
 
-    def unit(g, first_head, count, fresh):
+    def unit(g, first_head, count):
         columns = [pl.ds(pl.multiple_of((first_head + i) * HD, HD), HD) for i in range(count)]
         q = jnp.concatenate([queries[:, c] for c in columns], axis=0)
         do = jnp.concatenate([upstream[:, c] for c in columns], axis=0)
@@ -394,12 +394,8 @@
         weights_low = (raised * share).astype(BF16)
         key_terms = dot(grad_low, q, ((1,), (0,)))
         value_terms = dot(weights_low, do, ((1,), (0,)))
-        if fresh:
-            terms[2 * g] = key_terms
-            terms[2 * g + 1] = value_terms
-        else:
-            terms[2 * g] += key_terms
-            terms[2 * g + 1] += value_terms
+        terms[2 * g] = key_terms
+        terms[2 * g + 1] = value_terms
         back = dot(grad_low, k, ((0,), (0,)))
         for i, c in enumerate(columns):
             grad_query[:, c] = back[i * ROWS : (i + 1) * ROWS]
@@ -580,36 +576,33 @@
             handed[:, columns] = (upstream[:, columns].astype(F32) + inverse * grad_norm).astype(BF16)
         products[...] = total
 
-    half_group = per_group // 2
-
     def group_step(g):
         collect(g)
         assemble(g)
-        unit(g, g * per_group, half_group, True)
+        unit(g, g * per_group, per_group)
 
 
         @pl.when(g == 0)
         def _():
             forward(4, 3)
 
-        hand(g * per_group, half_group)
-        unit(g, g * per_group + half_group, half_group, False)
 
         send_far(g)
-        hand(g * per_group + half_group, half_group)
+
+        @pl.when(g >= 1)
+        def _():
+            pass_far(g - 1)
+
+        @pl.when(g >= 2)
+        def _():
+            send_mid(g - 2)
+
+        @pl.when(g >= 3)
+        def _():
+            send_near(g - 3)
+
+        hand(g * per_group, per_group)
         hand_copy(g).start()
-
-        @pl.when(g >= 1)
-        def _():
-            pass_far(g - 1)
-
-        @pl.when(g >= 2)
-        def _():
-            send_mid(g - 2)
-
-        @pl.when(g >= 3)
-        def _():
-            send_near(g - 3)
 
     each(0, groups, group_step)
 
@@ -654,7 +647,6 @@
         if g == 3:
             receive_hand()
             add_crosses()
-        send_near(g)
         if g == 1:
             for half in range(2):
                 start = terms[2 * (line[half] // 2) + half, half_rows(line[half])]
@@ -671,6 +663,8 @@
                     line_out[half] = line_sum[half].astype(BF16)
                     to = z * SIDE if half == 0 else y
                     cross_copy(line_out, cross_in, cross_send, cross_recv, half, cross[half], to).start()
+
+        send_near(g)
 
     @pl.when(device == 0)
     def _():

time: 74.2 us -> 73.3 us (0.988)
  Pallas kernels: 72.8 us -> 71.9 us
    pallas_call x1, Pallas kernels: 71.7 us -> 70.8 us  [on_device(): pl.pallas_call(body, name='relay', out_shape=(jax.ShapeDtypeStruct(stream...]
where the time goes in v5:
time: 73.3 us; the launch traced here: 73.2 us
  Pallas kernels  71.9 us (98%)
  between operations  1.29 us (2%)
    pallas_call x1, Pallas kernels, on_device(): pl.pallas_call(body, name='relay', out_shape=(jax.ShapeDtypeStruct(stream...  70.8 us

profile of v5, /device:TPU:6, one launch (start us, length us, event | category | flops | bytes accessed | tf_op | source)
XLA Modules:
  0.0 73.2 jit_solution(2854296413617104130)
XLA Ops:
  1.3 70.8 %relay.1 = (bf16[1,128,4096]{2,1,0:T(8,128)(2,1)S(1)}, bf16[1,128,512]{2,1,0:T(8,128)(2,1)S(1)}, bf16[1,128,512]{2,1,0:T(8,128)(2,1)S(1)}) custom-call(s32[1,1]{1,0:T(1,128)S(6)} %copy.9.refs_0_, f32[1,4096]{1,0:T(1,128)} %refs_1_.1, bf16[1,128,4096]{2,1,0:T(8,128)(2,1)} %refs_2_.1, bf16[1,128,4096]{2,1,0:T(8,128)(2,1)} %refs_3_.1, ...), custom_call_target="tpu_custom_call" | custom-call | tf_op jit(solution)/shard_map/relay/pallas_call | solution.py:763
  72.1 1.1 %write.1 = (bf16[1,128,4096]{2,1,0:T(8,128)(2,1)}, bf16[1,128,512]{2,1,0:T(8,128)(2,1)}, bf16[1,128,512]{2,1,0:T(8,128)(2,1)}) custom-call(bf16[1,128,4096]{2,1,0:T(8,128)(2,1)S(1)} %get-tuple-element.6.refs_0_, bf16[1,128,512]{2,1,0:T(8,128)(2,1)S(1)} %get-tuple-element.7.refs_1_, bf16[1,128,512]{2,1,0:T(8,128)(2,1)S(1)} %get-tuple-element.8.refs_2_), custom_call_target="tpu_custom_call" | custom-call | tf_op jit(solution)/shard_map/write/pallas_call | solution.py:845
